TPU v7x, 256 devices: a whole 4x4x8 slice. The times are simulated.
256 devices in a mesh: blk: 32 (over y, z), row: 8 (over x, core).
Axes of the slice: x: 4, y: 4, z: 8, core: 2. Of those that a mesh axis runs over, the one named last changes fastest.
Arguments:
- far_kernel: bfloat16 [256, 8, 512, 512], P('blk', None, 'row'), may hold values from -0.25 to 0.25
- near_kernel: bfloat16 [256, 2, 512, 512], P('blk', None, 'row'), may hold values from -0.25 to 0.25
- samples: bfloat16 [256, 512, 128], P('blk'), may hold values from -18 to 18
- far_target: int32 [256, 8], P('blk'), may hold values from 0 to 255, as said below
Outputs:
- basis_out: float32 [256, 512, 128], P('blk', 'row')
- coupling: float32 [256, 8, 128, 128], P('blk', None, 'row')
- parent_samples: float32 [128, 256, 128], P('blk', 'row')
Inputs may be any that keep to these rules, and one draw needn't show every extreme that they name: `far_target`: each row names 8 different target clusters; among the far blocks of the source clusters of one index of blk (rows 8 * g to 8 * g + 7), at most 4 name targets of any one index of blk (clusters 8 * h to 8 * h + 7), and exactly 4 for some such index.
All inputs are finite; a program needn't handle non-finite values.
Results may differ from a plain program's by a relative error of at most 0.02.
Values may be sent and summed in bfloat16 or wider, within the bound.
No kernel may reach another device: no remote copies, remote signals or barrier semaphores. Data moves between devices by JAX's collectives and lax.ppermute only.
A program may use at most 64 MiB of HBM per device.

v0:
```python
import functools

import jax
import jax.numpy as jnp
from jax import lax
from jax.experimental import pallas as pl
from jax.experimental.pallas import tpu as pltpu
from jax.sharding import Mesh, PartitionSpec as P

ITERS = 12
SLOTS = 4
META = 8
LIMIT = 61 << 20
ROOMY = 55 << 20
BF16 = jnp.bfloat16
F32 = jnp.float32
SMEM_SPEC = pl.BlockSpec(memory_space=pltpu.SMEM)
VMEM_SPEC = pl.BlockSpec(memory_space=pltpu.VMEM)
HBM_SPEC = pl.BlockSpec(memory_space=pl.ANY)
BLK = ("y", "z")
ROW = ("x", "core")


def in_vmem(value):
    return pltpu.with_memory_space_constraint(value, pltpu.VMEM)


def far_body(y_count, first, *refs):
    if first:
        place, target, far, samples, *send, slot_of, slot_id, buffer, count = refs
    else:
        slot_of, far, samples, *send, after, buffer = refs
    step = pl.program_id(0)
    pair, far_count, half, width = far.shape
    cols = buffer.shape[2]
    depth = buffer.shape[1]
    z_count = depth // (SLOTS * half)

    if first:

        @pl.when(step == 0)
        def _():
            for i in range(y_count * z_count):
                count[i] = 0
            for i in range(y_count * z_count * SLOTS):
                slot_id[i] = -1

    for i in range(pair):
        j = step * pair + i
        product = jnp.dot(far[i].reshape(far_count * half, width), samples[i], preferred_element_type=F32)
        product = product.astype(BF16).reshape(far_count, half, cols)
        for k in range(far_count):
            if first:
                local = target.shape[0]
                t = target[j, k]
                h = jnp.clip(t // local, 0, y_count * z_count - 1)
                g = (h // z_count + y_count - place[0]) % y_count * z_count + h % z_count
                c = jnp.minimum(count[g], SLOTS - 1)
                count[g] = c + 1
                q = g * SLOTS + c
                slot_of[j * far_count + k] = q
                slot_id[q] = t % local
            else:
                q = slot_of[j * far_count + k]
            start = pl.multiple_of(q % (z_count * SLOTS) * half, half)
            buffer[q // (z_count * SLOTS), pl.ds(start, half)] = product[k]

    @pl.when(step == pl.num_programs(0) - 1)
    def _():
        if first:
            row = lax.broadcasted_iota(jnp.int32, (META, cols), 0)
            lane = lax.broadcasted_iota(jnp.int32, (META, cols), 1) // (cols // SLOTS)
        if not first:
            after[0] = slot_of[0]
        for d in range(y_count):
            send[d][:depth] = buffer[d]
            if first and d:
                ids = jnp.full(row.shape, -1, jnp.int32)
                for z in range(z_count):
                    for c in range(SLOTS):
                        value = slot_id[(d * z_count + z) * SLOTS + c]
                        ids = jnp.where((row == z) & (lane == c), value, ids)
                send[d][depth:] = ids.astype(F32).astype(BF16)


def far_products(part, far_kernel, samples, y_count, z_count, *scalars):
    local, far_count, rows, width = far_kernel.shape
    cols = samples.shape[2]
    half = rows // 2
    first = part == 0
    depth = z_count * SLOTS * half
    pair = 2
    blocks = local * far_count
    sends = [pltpu.VMEM((depth + (META if first and d else 0), cols), BF16) for d in range(y_count)]
    tables = [jax.ShapeDtypeStruct((1,), jnp.int32)]
    scratch = [pltpu.VMEM((y_count, depth, cols), BF16)]
    if first:
        tables = [jax.ShapeDtypeStruct((n,), jnp.int32) for n in (blocks, y_count * z_count * SLOTS)]
        scratch += [pltpu.SMEM((y_count * z_count,), jnp.int32)]
    return pl.pallas_call(
        functools.partial(far_body, y_count, first),
        grid=(local // pair,),
        in_specs=[SMEM_SPEC] * len(scalars)
        + [
            pl.BlockSpec((pair, far_count, half, width), lambda j: (j, 0, part, 0)),
            pl.BlockSpec((pair, width, cols), lambda j: (j, 0, 0)),
        ],
        out_specs=[VMEM_SPEC] * y_count + [SMEM_SPEC] * len(tables),
        out_shape=sends + tables,
        scratch_shapes=scratch,
        cost_estimate=pl.CostEstimate(
            flops=blocks * rows * width * cols, bytes_accessed=4000000, transcendentals=0
        ),
        compiler_params=pltpu.CompilerParams(vmem_limit_bytes=LIMIT),
    )(*scalars, far_kernel, samples)


def near_body(near, samples, minus_near):
    for i in range(2):
        near_sum = jnp.dot(near[i, 0], samples[i], preferred_element_type=F32)
        near_sum += jnp.dot(near[i, 1], samples[1 - i], preferred_element_type=F32)
        minus_near[i] = -near_sum


def near_products(near_kernel, samples):
    local, _, rows, width = near_kernel.shape
    cols = samples.shape[2]
    return pl.pallas_call(
        near_body,
        grid=(local // 2,),
        in_specs=[
            pl.BlockSpec((2, 2, rows, width), lambda j: (j, 0, 0, 0)),
            pl.BlockSpec((2, width, cols), lambda j: (j, 0, 0)),
        ],
        out_specs=pl.BlockSpec((2, rows, cols), lambda j: (j, 0, 0)),
        out_shape=jax.ShapeDtypeStruct((local, rows, cols), F32),
        cost_estimate=pl.CostEstimate(
            flops=4 * local * rows * width * cols, bytes_accessed=2500000, transcendentals=0
        ),
        name="near_products",
    )(near_kernel, samples)


def collect_body(whole_array, ids, place, *refs):
    *refs, acc0, acc1, acc2, acc3 = refs
    partial = (acc0, acc1, acc2, acc3)
    y_count, z_count, _ = ids.shape
    received, dense = refs[:y_count], refs[y_count:]
    local, half, cols = acc0.shape[0] - 1, acc0.shape[1], acc0.shape[2]
    for i in range(z_count):
        z = i if whole_array else (place[0] + i) % z_count
        for acc in partial:
            acc[...] = jnp.zeros_like(acc)
        for d, block in enumerate(received):
            for c in range(SLOTS):
                at = ids[d, z, c]
                at = jnp.where((at < 0) | (at >= local), local, at)
                start = pl.multiple_of((z * SLOTS + c) * half, half)
                partial[c][at] = partial[c][at] + block[pl.ds(start, half)].astype(F32)
        total = acc0[:local] + acc1[:local] + acc2[:local] + acc3[:local]
        total = total.reshape(local * half, cols).astype(BF16)
        if whole_array:
            dense[0][i] = total
        else:
            dense[i][...] = total


def collect(part, ids, place, received, local, half):
    z_count = ids.shape[1]
    cols = received[0].shape[1]
    if part == 0:
        out = [jax.ShapeDtypeStruct((z_count, local * half, cols), BF16)]
    else:
        out = [pltpu.VMEM((local * half, cols), BF16)] * z_count
    return pl.pallas_call(
        functools.partial(collect_body, part == 0),
        in_specs=[SMEM_SPEC, SMEM_SPEC] + [VMEM_SPEC] * len(received),
        out_specs=[VMEM_SPEC] * len(out),
        out_shape=out,
        scratch_shapes=[pltpu.VMEM((local + 1, half, cols), F32)] * SLOTS,
        cost_estimate=pl.CostEstimate(flops=1000000, bytes_accessed=1600000, transcendentals=0),
        compiler_params=pltpu.CompilerParams(vmem_limit_bytes=LIMIT),
    )(ids, place, *[in_vmem(value) for value in received])


def dense_sum_body(first, *refs):
    *second, minus_near, sketch = refs
    local, rows, cols = sketch.shape
    half = rows // 2
    total = minus_near[:, :half]
    for z in range(first.shape[0]):
        total = total + first[z].astype(F32).reshape(local, half, cols)
    sketch[:, :half] = total.astype(BF16)
    total = minus_near[:, half:]
    for value in second:
        total = total + value[...].astype(F32).reshape(local, half, cols)
    sketch[:, half:] = total.astype(BF16)


def dense_sum(first, second, minus_near):
    return pl.pallas_call(
        dense_sum_body,
        in_specs=[VMEM_SPEC] * (2 + len(second)),
        out_specs=VMEM_SPEC,
        out_shape=pltpu.VMEM(minus_near.shape, BF16),
        cost_estimate=pl.CostEstimate(flops=1000000, bytes_accessed=1500000, transcendentals=0),
        compiler_params=pltpu.CompilerParams(vmem_limit_bytes=LIMIT),
        name="dense_sum",
    )(in_vmem(first), *[in_vmem(value) for value in second], minus_near)


def split(value):
    high = value.astype(BF16)
    return high, (value - high.astype(F32)).astype(BF16)


def left(parts):
    return jnp.concatenate(parts, axis=1)


def right(parts):
    row = jnp.concatenate(parts, axis=1)
    return jnp.concatenate([row, row], axis=0)


def product(a, b):
    both = jnp.dot(a, b, preferred_element_type=F32)
    cols = both.shape[1] // 2
    return both[:, :cols] + both[:, cols:]


def basis_body(sketch, basis_rows, basis_half):
    full_width, cols = basis_half.shape
    values = sketch[...].reshape(full_width, cols)
    gram = lax.dot_general(values, values, (((0,), (0,)), ((), ())), preferred_element_type=F32)
    identity = (
        lax.broadcasted_iota(jnp.int32, (cols, cols), 0) == lax.broadcasted_iota(jnp.int32, (cols, cols), 1)
    ).astype(F32)
    trace = jnp.sum(jnp.sum(gram * identity, axis=1, keepdims=True), axis=0, keepdims=True)
    mean_sq = trace / (full_width * cols) + 1e-6
    level = gram / (full_width * cols * mean_sq)
    root = 1.5 * identity - 0.5 * level
    step_parts = root_parts = split(root)
    level_parts = split(level)
    for i in range(ITERS - 1):
        level = product(left(level_parts), right(step_parts))
        if i:
            root = product(left(step_parts), right(root_parts))
        level_parts, root_parts = split(level), split(root)
        step_parts = split(1.5 * identity - 0.5 * product(left(root_parts), right(level_parts)))
    root = product(left(step_parts), right(root_parts)) / jnp.sqrt(cols * mean_sq)
    result = product(values, jnp.concatenate(split(root), axis=1)).astype(BF16)
    basis_half[...] = result
    basis_rows[...] = result.reshape(basis_rows.shape)


def basis_of(sketch):
    local, rows, cols = sketch.shape
    return pl.pallas_call(
        basis_body,
        in_specs=[VMEM_SPEC],
        out_specs=[VMEM_SPEC] * 2,
        out_shape=[pltpu.VMEM(sketch.shape, BF16), jax.ShapeDtypeStruct((local * rows, cols), BF16)],
        cost_estimate=pl.CostEstimate(flops=500000000, bytes_accessed=1000000, transcendentals=0),
        name="basis_of",
    )(in_vmem(sketch))


def spread_body(basis, first, second):
    local, rows, cols = basis.shape
    half = rows // 2
    values = basis[:, :half].reshape(local * half, cols)
    for z in range(first.shape[0]):
        first[z] = values
    second[...] = basis[:, half:].reshape(local * half, cols)


def spread(basis, z_count):
    local, rows, cols = basis.shape
    size = local * rows // 2
    return pl.pallas_call(
        spread_body,
        in_specs=[VMEM_SPEC],
        out_specs=[VMEM_SPEC] * 2,
        out_shape=[jax.ShapeDtypeStruct((z_count, size, cols), BF16), pltpu.VMEM((size, cols), BF16)],
        cost_estimate=pl.CostEstimate(flops=1000000, bytes_accessed=700000, transcendentals=0),
        name="spread",
    )(in_vmem(basis))


def pick_body(half, ids, place, *refs):
    y_count, z_count, _ = ids.shape
    bases, send = refs[:-y_count], refs[-y_count:]
    for i in range(z_count):
        z = i if len(bases) == 1 else (place[0] + z_count - i) % z_count
        source = bases[0].at[i] if len(bases) == 1 else bases[i]
        local = source.shape[0] // half
        for d, block in enumerate(send):
            for c in range(SLOTS):
                at = jnp.clip(ids[d, z, c], 0, local - 1)
                start = pl.multiple_of((z * SLOTS + c) * half, half)
                block[pl.ds(start, half)] = source[pl.ds(pl.multiple_of(at * half, half), half)]


def pick(ids, place, bases, half):
    y_count, z_count, _ = ids.shape
    cols = bases[0].shape[-1]
    return pl.pallas_call(
        functools.partial(pick_body, half),
        in_specs=[SMEM_SPEC, SMEM_SPEC] + [VMEM_SPEC] * len(bases),
        out_specs=[VMEM_SPEC] * y_count,
        out_shape=[pltpu.VMEM((z_count * SLOTS * half, cols), BF16)] * y_count,
        cost_estimate=pl.CostEstimate(flops=1000000, bytes_accessed=1600000, transcendentals=0),
        compiler_params=pltpu.CompilerParams(vmem_limit_bytes=ROOMY),
    )(ids, place, *[in_vmem(value) for value in bases])


def mixed_body(place, far, own, across, samples, mixed, parent, scratch):
    j = pl.program_id(0)
    far_count, rows, width = far.shape[1:]
    cols = own.shape[2]
    segment = jnp.where(j % 2 == place[0] % 2, own[0], across[0])
    values = jnp.dot(far[0].reshape(far_count * rows, width), segment, preferred_element_type=F32)
    mixed[pl.ds(j * far_count, far_count)] = values.astype(BF16).reshape(far_count, rows, cols)

    @pl.when(j % 2 == place[0] // 4)
    def _():
        scratch[...] = lax.dot_general(
            segment, samples[0], (((0,), (0,)), ((), ())), preferred_element_type=F32
        ) / jnp.sqrt(F32(width))
        count = parent.shape[1]
        start = pl.multiple_of((place[0] % 4) * count, count)
        parent[j // 2] = scratch[pl.ds(start, count)]


def mixed_products(place, far_kernel, own, across, samples):
    local, far_count, rows, width = far_kernel.shape
    x_count, _, cols = own.shape
    parent_rows = 2 * cols // local
    side = pl.BlockSpec(
        (1, width, cols), lambda j, place: ((place[0] // 2 + x_count - j // 2) % x_count, 0, 0)
    )
    return pl.pallas_call(
        mixed_body,
        grid_spec=pltpu.PrefetchScalarGridSpec(
            num_scalar_prefetch=1,
            grid=(local,),
            in_specs=[
                pl.BlockSpec((1, far_count, rows, width), lambda j, *_: (j, 0, 0, 0)),
                side,
                side,
                pl.BlockSpec((1, width, cols), lambda j, *_: (j, 0, 0)),
            ],
            out_specs=[VMEM_SPEC, VMEM_SPEC],
            scratch_shapes=[pltpu.VMEM((cols, cols), F32)],
        ),
        out_shape=[
            pltpu.VMEM((local * far_count, rows, cols), BF16),
            jax.ShapeDtypeStruct((local // 2, parent_rows, cols), F32),
        ],
        cost_estimate=pl.CostEstimate(
            flops=2 * local * far_count * rows * cols * width, bytes_accessed=8000000, transcendentals=0
        ),
        compiler_params=pltpu.CompilerParams(vmem_limit_bytes=ROOMY),
        name="mixed_products",
    )(place, far_kernel, own, across, samples)


def coupling_body(base, slot_of, place, mixed, *refs):
    if base:
        picked, mine, other = refs
    else:
        *received, mine, other, picked = refs
        y_count = picked.shape[1]
        for d in range(y_count):
            picked[0, d] = received[d][...]
            picked[1, d] = received[y_count + d][...]
    x_count, blocks, out_rows, cols = mine.shape
    rows = mixed.shape[1]
    half = rows // 2
    slots = picked.shape[2] // half
    zero = jnp.zeros((rows, cols), BF16)
    core = place[0] % 2
    for b in range(0, blocks, 2):
        basis_rows = []
        for i in range(2):
            q = slot_of[base + b + i]
            start = pl.multiple_of(q % slots * half, half)
            basis_rows += [picked[part, q // slots, pl.ds(start, half)] for part in range(2)]
        diagonal = jnp.concatenate(
            [
                jnp.concatenate([mixed[base + b], zero], axis=1),
                jnp.concatenate([zero, mixed[base + b + 1]], axis=1),
            ],
            axis=0,
        )
        both = lax.dot_general(
            jnp.concatenate(basis_rows, axis=0),
            diagonal,
            (((0,), (0,)), ((), ())),
            preferred_element_type=F32,
        )
        for i in range(2):
            part = both[:, i * cols : (i + 1) * cols].reshape(x_count, 2, out_rows, cols)
            for x in range(x_count):
                d = (x + x_count - place[0] // 2) % x_count
                mine[d, b + i] = jnp.where(core == 0, part[x, 0], part[x, 1]).astype(BF16)
                other[d, b + i] = jnp.where(core == 0, part[x, 1], part[x, 0]).astype(BF16)


def coupling_parts(part, slot_of, place, mixed, picked, x_count, local):
    blocks, rows, cols = mixed.shape
    shape = pltpu.VMEM((x_count, blocks // 2, cols // local, cols), BF16)
    again = [pltpu.VMEM((2, len(picked) // 2) + picked[0].shape, BF16)] if part == 0 else []
    return pl.pallas_call(
        functools.partial(coupling_body, part * blocks // 2),
        in_specs=[SMEM_SPEC, SMEM_SPEC] + [VMEM_SPEC] * (1 + len(picked)),
        out_specs=[VMEM_SPEC] * (2 + len(again)),
        out_shape=[shape, shape] + again,
        cost_estimate=pl.CostEstimate(
            flops=2 * blocks * rows * cols * cols, bytes_accessed=4000000, transcendentals=0
        ),
        compiler_params=pltpu.CompilerParams(vmem_limit_bytes=12 << 20),
    )(slot_of, place, in_vmem(mixed), *[in_vmem(value) for value in picked])


def pair_body(mine, partner, kept, *sent):
    kept[...] = mine[0].astype(F32) + partner[0].astype(F32)
    for d, out in enumerate(sent):
        out[...] = (mine[d + 1].astype(F32) + partner[d + 1].astype(F32)).astype(BF16)


def pair_sums(mine, partner):
    shape = mine.shape[1:]
    return pl.pallas_call(
        pair_body,
        in_specs=[VMEM_SPEC] * 2,
        out_specs=[VMEM_SPEC] * mine.shape[0],
        out_shape=[pltpu.VMEM(shape, F32)] + [pltpu.VMEM(shape, BF16)] * (mine.shape[0] - 1),
        cost_estimate=pl.CostEstimate(flops=1000000, bytes_accessed=1000000, transcendentals=0),
        compiler_params=pltpu.CompilerParams(vmem_limit_bytes=8 << 20),
    )(in_vmem(mine), in_vmem(partner))


def finish_body(scale, *refs):
    total = refs[0][...]
    for moved in refs[1:4]:
        total = total + moved[...].astype(F32)
    refs[-1][...] = total * scale


def finish(half, scale, parts, result):
    blocks, rows, cols = parts[0].shape
    before = [] if result is None else [result]
    return pl.pallas_call(
        functools.partial(finish_body, scale),
        grid=(1,),
        in_specs=[VMEM_SPEC] * len(parts) + [HBM_SPEC] * len(before),
        out_specs=pl.BlockSpec(parts[0].shape, lambda i: (half, 0, 0)),
        out_shape=jax.ShapeDtypeStruct((2 * blocks, rows, cols), F32),
        input_output_aliases={len(parts): 0} if before else {},
        cost_estimate=pl.CostEstimate(flops=1000000, bytes_accessed=1000000, transcendentals=0),
        compiler_params=pltpu.CompilerParams(vmem_limit_bytes=8 << 20),
    )(*[in_vmem(part) for part in parts], *before)


def per_device(far_kernel, near_kernel, samples, far_target):
    local, far_count, rows, width = far_kernel.shape
    cols = samples.shape[2]
    y_count, z_count = lax.axis_size("y"), lax.axis_size("z")
    half = rows // 2
    y_place, z_place = [lax.axis_index(name).astype(jnp.int32).reshape(1) for name in BLK]
    x_count = lax.axis_size("x")
    place = (lax.axis_index("x") * 2 + lax.axis_index("core")).astype(jnp.int32).reshape(1)

    def along_x(value, d):
        return lax.ppermute(value, "x", [(i, (i + d) % x_count) for i in range(x_count)])

    def shift(value, name, d, n):
        return lax.ppermute(value, name, [(i, (i + d) % n) for i in range(n)])

    *sent, slot_of, slot_id = far_products(
        0, far_kernel, samples, y_count, z_count, y_place, far_target
    )
    moved = [shift(sent[d], "y", d, y_count) for d in range(1, y_count)]
    *later, after = far_products(1, far_kernel, samples, y_count, z_count, slot_of)
    later = [later[0]] + [shift(later[d], "y", d, y_count) for d in range(1, y_count)]
    minus_near = near_products(near_kernel, samples)
    slot_id, after, minus_near = lax.optimization_barrier((slot_id, after, minus_near))
    slot_id = jnp.where(after < 0, -1, slot_id)
    depth = z_count * SLOTS * half
    ids = jnp.stack([value[depth:, :: cols // SLOTS] for value in moved]).astype(jnp.int32)
    ids = jnp.concatenate([slot_id[: z_count * SLOTS].reshape(1, z_count, SLOTS), ids])
    (dense,) = collect(0, ids, z_place, [sent[0]] + moved, local, half)
    first = lax.all_to_all(dense, "z", 0, 0, tiled=True)
    dense = collect(1, ids, z_place, later, local, half)
    order = sorted(range(1, z_count), key=lambda d: -min(d, z_count - d))
    second = [dense[0]] + [shift(dense[d], "z", d, z_count) for d in order]
    sketch = dense_sum(first, second, minus_near)
    sketch = lax.all_to_all(sketch, ROW, 0, 0, tiled=True)
    rows_sent, basis = basis_of(sketch)
    basis_rows = lax.all_to_all(rows_sent, ROW, 0, 0, tiled=True)
    first, second = spread(basis_rows, z_count)
    first = lax.all_to_all(first, "z", 0, 0, tiled=True)
    second = [second] + [shift(second, "z", d, z_count) for d in range(1, z_count)]
    chosen = pick(ids, z_place, [first], half)
    picked = [chosen[0]] + [shift(chosen[d], "y", -d, y_count) for d in range(1, y_count)]
    chosen = pick(ids, z_place, second, half)
    picked += [chosen[0]] + [shift(chosen[d], "y", -d, y_count) for d in range(1, y_count)]
    own = [along_x(basis, d) for d in range(1, x_count)]
    own = jnp.stack([basis] + own)
    own, basis_out = lax.optimization_barrier((own, basis_rows.astype(F32)))
    across = lax.ppermute(own, "core", [(0, 1), (1, 0)])
    mixed, parent = mixed_products(place, far_kernel, own, across, samples)
    coupling = None
    for part in range(2):
        mine, other, *again = coupling_parts(part, slot_of, place, mixed, picked, x_count, local)
        picked = again
        partner = lax.ppermute(other, "core", [(0, 1), (1, 0)])
        kept, *sent = pair_sums(mine, partner)
        parts = [kept] + [along_x(sent[d - 1], d) for d in range(1, x_count)]
        coupling = finish(part, width**-0.5, parts, coupling)
    return basis_out, coupling.reshape(local, far_count, cols // local, cols), parent


def solution(mesh):
    fine = Mesh(mesh.devices.reshape(4, 8, 4, 2), ("y", "z", "x", "core"))
    return jax.shard_map(
        per_device,
        mesh=fine,
        in_specs=(
            P(BLK, None, ROW, None),
            P(BLK, None, ROW, None),
            P(BLK, None, None),
            P(BLK, None),
        ),
        out_specs=(P(BLK, ROW, None), P(BLK, None, ROW, None), P(BLK, ROW, None)),
        check_vma=False,
    )
```

profile of v0, /device:TPU:1, one launch (start us, length us, event | category | flops | bytes accessed | tf_op | source)
XLA Modules:
  0.0 185.3 jit_solution(17508107997886699085)
XLA Ops:
  0.6 4.8 %shard_map.67 = (bf16[1024,128]{1,0:T(8,128)(2,1)S(1)}, bf16[1032,128]{1,0:T(8,128)(2,1)}, bf16[1032,128]{1,0:T(8,128)(2,1)S(1)}, bf16[1032,128]{1,0:T(8,128)(2,1)S(1)}, s32[64]{0:T(128)}, /*index=5*/s32[128]{0:T(128)}) custom-call(s32[1]{0:T(128)} %bitcast.refs_0_, s32[8,8]{1,0:T(8,128)} %refs_1_.2, bf16[8,8,64,512]{3,2,1,0:T(8,128)(2,1)} %far.1, ...), custom_call_target="tpu_custom_call" | custom-call | flops 268435456 | bytes 4000000 | tf_op jit(solution)/shard_map/pallas_call | solution.py:100
  5.4 2.2 %collective-permute-start = (bf16[1032,128]{1,0:T(8,128)(2,1)}, bf16[1032,128]{1,0:T(8,128)(2,1)S(1)}, u32[]{:S(2)}, u32[]{:S(2)}) collective-permute-start(bf16[1032,128]{1,0:T(8,128)(2,1)} %get-tuple-element.59), channel_id=1, source_target_pairs={{0,64},{64,128},{128,192},{192,0},{1,65},{65,129},{129,193},{193,1... | collective-permute-start | bytes 792584 | tf_op jit(solution)/shard_map/ppermute | solution.py:480
  7.6 2.6 %collective-permute-start.1 = (bf16[1032,128]{1,0:T(8,128)(2,1)S(1)}, bf16[1032,128]{1,0:T(8,128)(2,1)S(1)}, u32[]{:S(2)}, u32[]{:S(2)}) collective-permute-start(bf16[1032,128]{1,0:T(8,128)(2,1)S(1)} %get-tuple-element.60), channel_id=1, source_target_pairs={{0,128},{64,192},{128,0},{192,64},{1,129},{65,193},{129,1},{193,65... | collective-permute-start | bytes 792584 | tf_op jit(solution)/shard_map/ppermute | solution.py:480
  10.2 1.1 collective-permute-start.2
  11.3 3.8 %near_products.1.refs_8_ = f32[8,64,128]{2,1,0:T(8,128)} custom-call(bf16[8,2,64,512]{3,2,1,0:T(8,128)(2,1)} %near.1, bf16[8,512,128]{2,1,0:T(8,128)(2,1)} %samples.3), custom_call_target="tpu_custom_call" | custom-call | flops 134217728 | bytes 2500000 | tf_op jit(solution)/shard_map/near_products/pallas_call | solution.py:128
  15.1 4.1 %shard_map.68 = (bf16[1024,128]{1,0:T(8,128)(2,1)S(1)}, bf16[1024,128]{1,0:T(8,128)(2,1)}, bf16[1024,128]{1,0:T(8,128)(2,1)}, bf16[1024,128]{1,0:T(8,128)(2,1)S(1)}, s32[1]{0:T(128)}) custom-call(s32[64]{0:T(128)} %get-tuple-element.55.refs_0_.slot_of, bf16[8,8,64,512]{3,2,1,0:T(8,128)(2,1)} %far.1, bf16[8,512,128]{2,1,0:T(8,128)(2,1)} %samples.3), custom_call_target="tpu_custom_call" | custom-call | flops 268435456 | bytes 4000000 | tf_op jit(solution)/shard_map/pallas_call | solution.py:100
  20.0 1.8 collective-permute-done.1.refs_2_
  22.7 2.3 %shard_map.69 = bf16[8,256,128]{2,1,0:T(8,128)(2,1)} custom-call(s32[4,8,4]{2,1,0:T(8,128)} %pad_add_fusion.ids, s32[1]{0:T(128)} %bitcast.5.place, bf16[1024,128]{1,0:T(8,128)(2,1)S(1)} %get-tuple-element.62.refs_0_, bf16[1032,128]{1,0:T(8,128)(2,1)S(1)} %collective-permute-done.refs_1_, bf16[1032,128]{1,0:T(8,128)(2,1)S(1)} %collective-permute-done.1.refs_2_, ...), custom_call_target="tpu_custom_call" | custom-call | flops 1000000 | bytes 1600000 | tf_op jit(solution)/shard_map/pallas_call | solution.py:175
  25.0 8.2 %all-to-all-start = ((bf16[8,256,128]{2,1,0:T(8,128)(2,1)}), bf16[8,256,128]{2,1,0:T(8,128)(2,1)S(1)}, u32[]{:S(2)}, u32[]{:S(2)}) async-start(bf16[8,256,128]{2,1,0:T(8,128)(2,1)} %shard_map.69), calls=%async_computation | async-start | bytes 1048576 | tf_op jit(solution)/shard_map/all_to_all | solution.py:495
  33.2 1.0 collective-permute-start.3
  34.2 2.8 %collective-permute-start.4 = (bf16[1024,128]{1,0:T(8,128)(2,1)}, bf16[1024,128]{1,0:T(8,128)(2,1)S(1)}, u32[]{:S(2)}, u32[]{:S(2)}) collective-permute-start(bf16[1024,128]{1,0:T(8,128)(2,1)} %get-tuple-element.65), channel_id=1, source_target_pairs={{0,128},{64,192},{128,0},{192,64},{1,129},{65,193},{129,1},{193,65... | collective-permute-start | bytes 786440 | tf_op jit(solution)/shard_map/ppermute | solution.py:480
  37.0 3.7 %collective-permute-done.3.refs_1_ = bf16[1024,128]{1,0:T(8,128)(2,1)S(1)} collective-permute-done((bf16[1024,128]{1,0:T(8,128)(2,1)}, bf16[1024,128]{1,0:T(8,128)(2,1)S(1)}, u32[]{:S(2)}, u32[]{:S(2)}) %collective-permute-start.3) | collective-permute-done | bytes 262176 | tf_op jit(solution)/shard_map/ppermute | solution.py:480
  40.6 7.8 %collective-permute-done.4.refs_2_ = bf16[1024,128]{1,0:T(8,128)(2,1)S(1)} collective-permute-done((bf16[1024,128]{1,0:T(8,128)(2,1)}, bf16[1024,128]{1,0:T(8,128)(2,1)S(1)}, u32[]{:S(2)}, u32[]{:S(2)}) %collective-permute-start.4) | collective-permute-done | bytes 262176 | tf_op jit(solution)/shard_map/ppermute | solution.py:480
  48.4 1.5 shard_map.70
  49.9 5.2 %collective-permute-start.6 = (bf16[256,128]{1,0:T(8,128)(2,1)S(1)}, bf16[256,128]{1,0:T(8,128)(2,1)S(1)}, u32[]{:S(2)}, u32[]{:S(2)}) collective-permute-start(bf16[256,128]{1,0:T(8,128)(2,1)S(1)} %get-tuple-element.68), channel_id=1, source_target_pairs={{0,32},{8,40},{16,48},{24,56},{32,0},{40,8},{48,16},{56,24},{1,33}... | collective-permute-start | bytes 196616 | tf_op jit(solution)/shard_map/ppermute | solution.py:480
  55.4 4.2 %collective-permute-start.8 = (bf16[256,128]{1,0:T(8,128)(2,1)S(1)}, bf16[256,128]{1,0:T(8,128)(2,1)S(1)}, u32[]{:S(2)}, u32[]{:S(2)}) collective-permute-start(bf16[256,128]{1,0:T(8,128)(2,1)S(1)} %get-tuple-element.70), channel_id=1, source_target_pairs={{0,40},{8,48},{16,56},{24,0},{32,8},{40,16},{48,24},{56,32},{1,41}... | collective-permute-start | bytes 196616 | tf_op jit(solution)/shard_map/ppermute | solution.py:480
  59.9 3.3 %collective-permute-start.10 = (bf16[256,128]{1,0:T(8,128)(2,1)S(1)}, bf16[256,128]{1,0:T(8,128)(2,1)S(1)}, u32[]{:S(2)}, u32[]{:S(2)}) collective-permute-start(bf16[256,128]{1,0:T(8,128)(2,1)S(1)} %get-tuple-element.72), channel_id=1, source_target_pairs={{0,48},{8,56},{16,0},{24,8},{32,16},{40,24},{48,32},{56,40},{1,49}... | collective-permute-start | bytes 196616 | tf_op jit(solution)/shard_map/ppermute | solution.py:480
  63.4 2.4 %collective-permute-start.12 = (bf16[256,128]{1,0:T(8,128)(2,1)S(1)}, bf16[256,128]{1,0:T(8,128)(2,1)S(1)}, u32[]{:S(2)}, u32[]{:S(2)}) collective-permute-start(bf16[256,128]{1,0:T(8,128)(2,1)S(1)} %get-tuple-element.74), channel_id=1, source_target_pairs={{0,56},{8,0},{16,8},{24,16},{32,24},{40,32},{48,40},{56,48},{1,57}... | collective-permute-start | bytes 196616 | tf_op jit(solution)/shard_map/ppermute | solution.py:480
  65.8 0.7 collective-permute-done.10.refs_5_
  66.6 2.2 %collective-permute-done.11.refs_6_ = bf16[256,128]{1,0:T(8,128)(2,1)S(1)} collective-permute-done((bf16[256,128]{1,0:T(8,128)(2,1)S(1)}, bf16[256,128]{1,0:T(8,128)(2,1)S(1)}, u32[]{:S(2)}, u32[]{:S(2)}) %collective-permute-start.11) | collective-permute-done | bytes 65568 | tf_op jit(solution)/shard_map/ppermute | solution.py:480
  68.8 1.1 dense_sum.1
  69.9 12.5 %all_to_all.20.sketch = bf16[8,64,128]{2,1,0:T(8,128)(2,1)S(1)} all-to-all(bf16[8,64,128]{2,1,0:T(8,128)(2,1)S(1)} %dense_sum.1), channel_id=1, replica_groups=mesh['y'=4,'z'=8,'x'=4,'core'=2] {'x','core'}, dimensions={0} | all-to-all | bytes 262144 | tf_op jit(solution)/shard_map/all_to_all | solution.py:500
  82.4 5.1 %basis_of.1 = (bf16[8,64,128]{2,1,0:T(8,128)(2,1)S(1)}, bf16[512,128]{1,0:T(8,128)(2,1)}) custom-call(bf16[8,64,128]{2,1,0:T(8,128)(2,1)S(1)} %all_to_all.20.sketch), custom_call_target="tpu_custom_call" | custom-call | flops 500000000 | bytes 1000000 | tf_op jit(solution)/shard_map/basis_of/pallas_call | solution.py:259
  87.5 8.5 %all_to_all.21.basis = bf16[8,64,128]{2,1,0:T(8,128)(2,1)S(1)} all-to-all(bf16[8,64,128]{2,1,0:T(8,128)(2,1)S(1)} %get-tuple-element.77), channel_id=1, replica_groups=mesh['y'=4,'z'=8,'x'=4,'core'=2] {'x','core'}, dimensions={0} | all-to-all | bytes 262144 | tf_op jit(solution)/shard_map/all_to_all | solution.py:502
  96.0 0.9 spread.1
  96.9 4.2 %all-to-all-start.3 = ((bf16[8,256,128]{2,1,0:T(8,128)(2,1)}), bf16[8,256,128]{2,1,0:T(8,128)(2,1)S(1)}, u32[]{:S(2)}, u32[]{:S(2)}) async-start(bf16[8,256,128]{2,1,0:T(8,128)(2,1)} %get-tuple-element.81), calls=%async_computation.3 | async-start | bytes 1048576 | tf_op jit(solution)/shard_map/all_to_all | solution.py:504
  101.1 0.9 collective-permute-start.15
  102.0 1.2 collective-permute-start.14
  103.2 0.7 convert_element_type.7
  103.9 1.2 collective-permute-done.15
  105.1 2.4 %collective-permute-done.14 = bf16[512,128]{1,0:T(8,128)(2,1)S(1)} collective-permute-done((bf16[512,128]{1,0:T(8,128)(2,1)}, bf16[512,128]{1,0:T(8,128)(2,1)S(1)}, u32[]{:S(2)}, u32[]{:S(2)}) %collective-permute-start.14) | collective-permute-done | bytes 131104 | tf_op jit(solution)/shard_map/ppermute | solution.py:477
  107.5 3.4 %collective-permute-done.13 = bf16[512,128]{1,0:T(8,128)(2,1)S(1)} collective-permute-done((bf16[512,128]{1,0:T(8,128)(2,1)}, bf16[512,128]{1,0:T(8,128)(2,1)S(1)}, u32[]{:S(2)}, u32[]{:S(2)}) %collective-permute-start.13) | collective-permute-done | bytes 131104 | tf_op jit(solution)/shard_map/ppermute | solution.py:477
  110.9 1.8 pad_maximum_fusion.own
  112.7 1.5 collective-permute-start.16
  114.2 2.7 %collective-permute-start.26 = (bf16[256,128]{1,0:T(8,128)(2,1)S(1)}, bf16[256,128]{1,0:T(8,128)(2,1)S(1)}, u32[]{:S(2)}, u32[]{:S(2)}) collective-permute-start(bf16[256,128]{1,0:T(8,128)(2,1)S(1)} %get-tuple-element.86.refs_0_), channel_id=1, source_target_pairs={{0,56},{8,0},{16,8},{24,16},{32,24},{40,32},{48,40},{56,48},{1,57}... | collective-permute-start | bytes 196616 | tf_op jit(solution)/shard_map/ppermute | solution.py:480
  116.8 2.1 %collective-permute-start.25 = (bf16[256,128]{1,0:T(8,128)(2,1)S(1)}, bf16[256,128]{1,0:T(8,128)(2,1)S(1)}, u32[]{:S(2)}, u32[]{:S(2)}) collective-permute-start(bf16[256,128]{1,0:T(8,128)(2,1)S(1)} %get-tuple-element.86.refs_0_), channel_id=1, source_target_pairs={{0,48},{8,56},{16,0},{24,8},{32,16},{40,24},{48,32},{56,40},{1,49}... | collective-permute-start | bytes 196616 | tf_op jit(solution)/shard_map/ppermute | solution.py:480
  118.9 1.2 collective-permute-start.24
  120.1 3.3 %collective-permute-start.23 = (bf16[256,128]{1,0:T(8,128)(2,1)S(1)}, bf16[256,128]{1,0:T(8,128)(2,1)S(1)}, u32[]{:S(2)}, u32[]{:S(2)}) collective-permute-start(bf16[256,128]{1,0:T(8,128)(2,1)S(1)} %get-tuple-element.86.refs_0_), channel_id=1, source_target_pairs={{0,32},{8,40},{16,48},{24,56},{32,0},{40,8},{48,16},{56,24},{1,33}... | collective-permute-start | bytes 196616 | tf_op jit(solution)/shard_map/ppermute | solution.py:480
  123.4 3.3 %collective-permute-start.21 = (bf16[256,128]{1,0:T(8,128)(2,1)S(1)}, bf16[256,128]{1,0:T(8,128)(2,1)S(1)}, u32[]{:S(2)}, u32[]{:S(2)}) collective-permute-start(bf16[256,128]{1,0:T(8,128)(2,1)S(1)} %get-tuple-element.86.refs_0_), channel_id=1, source_target_pairs={{0,16},{8,24},{16,32},{24,40},{32,48},{40,56},{48,0},{56,8},{1,17}... | collective-permute-start | bytes 196616 | tf_op jit(solution)/shard_map/ppermute | solution.py:480
  126.7 1.2 collective-permute-start.20
  127.9 5.1 %collective-permute-done.22.refs_3_ = bf16[256,128]{1,0:T(8,128)(2,1)S(1)} collective-permute-done((bf16[256,128]{1,0:T(8,128)(2,1)S(1)}, bf16[256,128]{1,0:T(8,128)(2,1)S(1)}, u32[]{:S(2)}, u32[]{:S(2)}) %collective-permute-start.22) | collective-permute-done | bytes 65568 | tf_op jit(solution)/shard_map/ppermute | solution.py:480
  133.0 2.7 %collective-permute-done.21.refs_2_ = bf16[256,128]{1,0:T(8,128)(2,1)S(1)} collective-permute-done((bf16[256,128]{1,0:T(8,128)(2,1)S(1)}, bf16[256,128]{1,0:T(8,128)(2,1)S(1)}, u32[]{:S(2)}, u32[]{:S(2)}) %collective-permute-start.21) | collective-permute-done | bytes 65568 | tf_op jit(solution)/shard_map/ppermute | solution.py:480
  135.7 0.8 collective-permute-done.20.refs_1_
  136.4 1.4 shard_map.72
  137.8 2.0 %collective-permute-start.27 = (bf16[1024,128]{1,0:T(8,128)(2,1)S(1)}, bf16[1024,128]{1,0:T(8,128)(2,1)S(1)}, u32[]{:S(2)}, u32[]{:S(2)}) collective-permute-start(bf16[1024,128]{1,0:T(8,128)(2,1)S(1)} %get-tuple-element.88), channel_id=1, source_target_pairs={{0,192},{64,0},{128,64},{192,128},{1,193},{65,1},{129,65},{193,129... | collective-permute-start | bytes 786440 | tf_op jit(solution)/shard_map/ppermute | solution.py:480
  139.8 0.9 collective-permute-start.28
  140.7 1.3 shard_map.71
  142.0 2.8 %collective-permute-start.17 = (bf16[1024,128]{1,0:T(8,128)(2,1)S(1)}, bf16[1024,128]{1,0:T(8,128)(2,1)S(1)}, u32[]{:S(2)}, u32[]{:S(2)}) collective-permute-start(bf16[1024,128]{1,0:T(8,128)(2,1)S(1)} %get-tuple-element.83), channel_id=1, source_target_pairs={{0,192},{64,0},{128,64},{192,128},{1,193},{65,1},{129,65},{193,129... | collective-permute-start | bytes 786440 | tf_op jit(solution)/shard_map/ppermute | solution.py:480
  144.7 1.8 collective-permute-start.18
  146.5 2.5 %collective-permute-start.19 = (bf16[1024,128]{1,0:T(8,128)(2,1)S(1)}, bf16[1024,128]{1,0:T(8,128)(2,1)S(1)}, u32[]{:S(2)}, u32[]{:S(2)}) collective-permute-start(bf16[1024,128]{1,0:T(8,128)(2,1)S(1)} %get-tuple-element.85), channel_id=1, source_target_pairs={{0,64},{64,128},{128,192},{192,0},{1,65},{65,129},{129,193},{193,1... | collective-permute-start | bytes 786440 | tf_op jit(solution)/shard_map/ppermute | solution.py:480
  149.0 7.7 %mixed_products.1 = (bf16[64,64,128]{2,1,0:T(8,128)(2,1)S(1)}, f32[4,32,128]{2,1,0:T(8,128)}) custom-call(s32[1]{0:T(128)} %bitcast.10.place, bf16[8,8,64,512]{3,2,1,0:T(8,128)(2,1)} %far.1, bf16[4,512,128]{2,1,0:T(8,128)(2,1)} %pad_maximum_fusion.own, bf16[4,512,128]{2,1,0:T(8,128)(2,1)} %collective-permute-done.16.across, bf16[8,512,128]{2,1,0:T(8,128)(2,1)} %samples.3), custom_call_target="tpu_custom_call" | custom-call | flops 536870912 | bytes 8000000 | tf_op jit(solution)/shard_map/mixed_products/pallas_call | solution.py:343
  157.0 1.2 collective-permute-done.18.refs_2_
  158.2 8.2 %collective-permute-done.19.refs_3_ = bf16[1024,128]{1,0:T(8,128)(2,1)S(1)} collective-permute-done((bf16[1024,128]{1,0:T(8,128)(2,1)S(1)}, bf16[1024,128]{1,0:T(8,128)(2,1)S(1)}, u32[]{:S(2)}, u32[]{:S(2)}) %collective-permute-start.19) | collective-permute-done | bytes 262176 | tf_op jit(solution)/shard_map/ppermute | solution.py:480
  166.4 1.1 shard_map.73
  167.5 0.6 collective-permute-start.34
  168.2 1.1 shard_map.74
  169.9 1.4 collective-permute-start.36
  171.4 1.8 collective-permute-start.37
  173.4 1.9 %collective-permute-start.32 = (bf16[32,16,128]{2,1,0:T(8,128)(2,1)S(1)}, bf16[32,16,128]{2,1,0:T(8,128)(2,1)S(1)}, u32[]{:S(2)}, u32[]{:S(2)}) collective-permute-start(bf16[32,16,128]{2,1,0:T(8,128)(2,1)S(1)} %get-tuple-element.96), channel_id=1, source_target_pairs={{0,4},{2,6},{4,0},{6,2},{1,5},{3,7},{5,1},{7,3},{8,12},{10,14},{12... | collective-permute-start | bytes 393224 | tf_op jit(solution)/shard_map/ppermute | solution.py:477
  175.2 2.9 %collective-permute-done.35.refs_1_ = bf16[32,16,128]{2,1,0:T(8,128)(2,1)S(1)} collective-permute-done((bf16[32,16,128]{2,1,0:T(8,128)(2,1)S(1)}, bf16[32,16,128]{2,1,0:T(8,128)(2,1)S(1)}, u32[]{:S(2)}, u32[]{:S(2)}) %collective-permute-start.35) | collective-permute-done | bytes 131104 | tf_op jit(solution)/shard_map/ppermute | solution.py:477
  178.2 1.2 collective-permute-done.37.refs_3_
  179.4 0.8 shard_map.77.refs_4_
  180.2 4.1 %collective-permute-done.31.refs_1_ = bf16[32,16,128]{2,1,0:T(8,128)(2,1)S(1)} collective-permute-done((bf16[32,16,128]{2,1,0:T(8,128)(2,1)S(1)}, bf16[32,16,128]{2,1,0:T(8,128)(2,1)S(1)}, u32[]{:S(2)}, u32[]{:S(2)}) %collective-permute-start.31) | collective-permute-done | bytes 131104 | tf_op jit(solution)/shard_map/ppermute | solution.py:477
  184.5 0.8 shard_map.78
  (48 shorter events, 3.3 us)
Async XLA Ops:
  5.4 14.4 %copy-start.1 = (s32[128]{0:T(128)S(1)}, s32[128]{0:T(128)}, u32[]{:S(2)}) copy-start(s32[128]{0:T(128)} %get-tuple-element.58) | copy-start | bytes 1540
  5.4 14.5 %collective-permute-start = (bf16[1032,128]{1,0:T(8,128)(2,1)}, bf16[1032,128]{1,0:T(8,128)(2,1)S(1)}, u32[]{:S(2)}, u32[]{:S(2)}) collective-permute-start(bf16[1032,128]{1,0:T(8,128)(2,1)} %get-tuple-element.59), channel_id=1, source_target_pairs={{0,64},{64,128},{128,192},{192,0},{1,65},{65,129},{129,193},{193,1... | collective-permute-start | bytes 792584 | tf_op jit(solution)/shard_map/ppermute | solution.py:480
  7.6 14.2 %collective-permute-start.1 = (bf16[1032,128]{1,0:T(8,128)(2,1)S(1)}, bf16[1032,128]{1,0:T(8,128)(2,1)S(1)}, u32[]{:S(2)}, u32[]{:S(2)}) collective-permute-start(bf16[1032,128]{1,0:T(8,128)(2,1)S(1)} %get-tuple-element.60), channel_id=1, source_target_pairs={{0,128},{64,192},{128,0},{192,64},{1,129},{65,193},{129,1},{193,65... | collective-permute-start | bytes 792584 | tf_op jit(solution)/shard_map/ppermute | solution.py:480
  10.2 11.7 %collective-permute-start.2 = (bf16[1032,128]{1,0:T(8,128)(2,1)S(1)}, bf16[1032,128]{1,0:T(8,128)(2,1)S(1)}, u32[]{:S(2)}, u32[]{:S(2)}) collective-permute-start(bf16[1032,128]{1,0:T(8,128)(2,1)S(1)} %get-tuple-element.61), channel_id=1, source_target_pairs={{0,192},{64,0},{128,64},{192,128},{1,193},{65,1},{129,65},{193,129... | collective-permute-start | bytes 792584 | tf_op jit(solution)/shard_map/ppermute | solution.py:480
  25.0 43.8 %all-to-all-start = ((bf16[8,256,128]{2,1,0:T(8,128)(2,1)}), bf16[8,256,128]{2,1,0:T(8,128)(2,1)S(1)}, u32[]{:S(2)}, u32[]{:S(2)}) async-start(bf16[8,256,128]{2,1,0:T(8,128)(2,1)} %shard_map.69), calls=%async_computation | async-start | bytes 1048576 | tf_op jit(solution)/shard_map/all_to_all | solution.py:495
  33.2 7.5 %collective-permute-start.3 = (bf16[1024,128]{1,0:T(8,128)(2,1)}, bf16[1024,128]{1,0:T(8,128)(2,1)S(1)}, u32[]{:S(2)}, u32[]{:S(2)}) collective-permute-start(bf16[1024,128]{1,0:T(8,128)(2,1)} %get-tuple-element.64), channel_id=1, source_target_pairs={{0,64},{64,128},{128,192},{192,0},{1,65},{65,129},{129,193},{193,1... | collective-permute-start | bytes 786440 | tf_op jit(solution)/shard_map/ppermute | solution.py:480
  34.2 14.2 %collective-permute-start.4 = (bf16[1024,128]{1,0:T(8,128)(2,1)}, bf16[1024,128]{1,0:T(8,128)(2,1)S(1)}, u32[]{:S(2)}, u32[]{:S(2)}) collective-permute-start(bf16[1024,128]{1,0:T(8,128)(2,1)} %get-tuple-element.65), channel_id=1, source_target_pairs={{0,128},{64,192},{128,0},{192,64},{1,129},{65,193},{129,1},{193,65... | collective-permute-start | bytes 786440 | tf_op jit(solution)/shard_map/ppermute | solution.py:480
  37.0 11.5 %collective-permute-start.5 = (bf16[1024,128]{1,0:T(8,128)(2,1)S(1)}, bf16[1024,128]{1,0:T(8,128)(2,1)S(1)}, u32[]{:S(2)}, u32[]{:S(2)}) collective-permute-start(bf16[1024,128]{1,0:T(8,128)(2,1)S(1)} %get-tuple-element.66), channel_id=1, source_target_pairs={{0,192},{64,0},{128,64},{192,128},{1,193},{65,1},{129,65},{193,129... | collective-permute-start | bytes 786440 | tf_op jit(solution)/shard_map/ppermute | solution.py:480
  49.9 13.2 %collective-permute-start.6 = (bf16[256,128]{1,0:T(8,128)(2,1)S(1)}, bf16[256,128]{1,0:T(8,128)(2,1)S(1)}, u32[]{:S(2)}, u32[]{:S(2)}) collective-permute-start(bf16[256,128]{1,0:T(8,128)(2,1)S(1)} %get-tuple-element.68), channel_id=1, source_target_pairs={{0,32},{8,40},{16,48},{24,56},{32,0},{40,8},{48,16},{56,24},{1,33}... | collective-permute-start | bytes 196616 | tf_op jit(solution)/shard_map/ppermute | solution.py:480
  55.1 8.3 %collective-permute-start.7 = (bf16[256,128]{1,0:T(8,128)(2,1)S(1)}, bf16[256,128]{1,0:T(8,128)(2,1)S(1)}, u32[]{:S(2)}, u32[]{:S(2)}) collective-permute-start(bf16[256,128]{1,0:T(8,128)(2,1)S(1)} %get-tuple-element.69), channel_id=1, source_target_pairs={{0,24},{8,32},{16,40},{24,48},{32,56},{40,0},{48,8},{56,16},{1,25}... | collective-permute-start | bytes 196616 | tf_op jit(solution)/shard_map/ppermute | solution.py:480
  55.4 10.5 %collective-permute-start.8 = (bf16[256,128]{1,0:T(8,128)(2,1)S(1)}, bf16[256,128]{1,0:T(8,128)(2,1)S(1)}, u32[]{:S(2)}, u32[]{:S(2)}) collective-permute-start(bf16[256,128]{1,0:T(8,128)(2,1)S(1)} %get-tuple-element.70), channel_id=1, source_target_pairs={{0,40},{8,48},{16,56},{24,0},{32,8},{40,16},{48,24},{56,32},{1,41}... | collective-permute-start | bytes 196616 | tf_op jit(solution)/shard_map/ppermute | solution.py:480
  59.6 6.3 %collective-permute-start.9 = (bf16[256,128]{1,0:T(8,128)(2,1)S(1)}, bf16[256,128]{1,0:T(8,128)(2,1)S(1)}, u32[]{:S(2)}, u32[]{:S(2)}) collective-permute-start(bf16[256,128]{1,0:T(8,128)(2,1)S(1)} %get-tuple-element.71), channel_id=1, source_target_pairs={{0,16},{8,24},{16,32},{24,40},{32,48},{40,56},{48,0},{56,8},{1,17}... | collective-permute-start | bytes 196616 | tf_op jit(solution)/shard_map/ppermute | solution.py:480
  59.9 6.7 %collective-permute-start.10 = (bf16[256,128]{1,0:T(8,128)(2,1)S(1)}, bf16[256,128]{1,0:T(8,128)(2,1)S(1)}, u32[]{:S(2)}, u32[]{:S(2)}) collective-permute-start(bf16[256,128]{1,0:T(8,128)(2,1)S(1)} %get-tuple-element.72), channel_id=1, source_target_pairs={{0,48},{8,56},{16,0},{24,8},{32,16},{40,24},{48,32},{56,40},{1,49}... | collective-permute-start | bytes 196616 | tf_op jit(solution)/shard_map/ppermute | solution.py:480
  63.2 5.6 %collective-permute-start.11 = (bf16[256,128]{1,0:T(8,128)(2,1)S(1)}, bf16[256,128]{1,0:T(8,128)(2,1)S(1)}, u32[]{:S(2)}, u32[]{:S(2)}) collective-permute-start(bf16[256,128]{1,0:T(8,128)(2,1)S(1)} %get-tuple-element.73), channel_id=1, source_target_pairs={{0,8},{8,16},{16,24},{24,32},{32,40},{40,48},{48,56},{56,0},{1,9},... | collective-permute-start | bytes 196616 | tf_op jit(solution)/shard_map/ppermute | solution.py:480
  63.4 5.3 %collective-permute-start.12 = (bf16[256,128]{1,0:T(8,128)(2,1)S(1)}, bf16[256,128]{1,0:T(8,128)(2,1)S(1)}, u32[]{:S(2)}, u32[]{:S(2)}) collective-permute-start(bf16[256,128]{1,0:T(8,128)(2,1)S(1)} %get-tuple-element.74), channel_id=1, source_target_pairs={{0,56},{8,0},{16,8},{24,16},{32,24},{40,32},{48,40},{56,48},{1,57}... | collective-permute-start | bytes 196616 | tf_op jit(solution)/shard_map/ppermute | solution.py:480
  96.9 43.8 %all-to-all-start.3 = ((bf16[8,256,128]{2,1,0:T(8,128)(2,1)}), bf16[8,256,128]{2,1,0:T(8,128)(2,1)S(1)}, u32[]{:S(2)}, u32[]{:S(2)}) async-start(bf16[8,256,128]{2,1,0:T(8,128)(2,1)} %get-tuple-element.81), calls=%async_computation.3 | async-start | bytes 1048576 | tf_op jit(solution)/shard_map/all_to_all | solution.py:504
  101.1 4.0 %collective-permute-start.15 = (bf16[512,128]{1,0:T(8,128)(2,1)}, bf16[512,128]{1,0:T(8,128)(2,1)S(1)}, u32[]{:S(2)}, u32[]{:S(2)}) collective-permute-start(bf16[512,128]{1,0:T(8,128)(2,1)} %get-tuple-element.76), channel_id=1, source_target_pairs={{0,6},{2,0},{4,2},{6,4},{1,7},{3,1},{5,3},{7,5},{8,14},{10,8},{12,... | collective-permute-start | bytes 393224 | tf_op jit(solution)/shard_map/ppermute | solution.py:477
  102.0 5.6 %collective-permute-start.14 = (bf16[512,128]{1,0:T(8,128)(2,1)}, bf16[512,128]{1,0:T(8,128)(2,1)S(1)}, u32[]{:S(2)}, u32[]{:S(2)}) collective-permute-start(bf16[512,128]{1,0:T(8,128)(2,1)} %get-tuple-element.76), channel_id=1, source_target_pairs={{0,4},{2,6},{4,0},{6,2},{1,5},{3,7},{5,1},{7,3},{8,12},{10,14},{12... | collective-permute-start | bytes 393224 | tf_op jit(solution)/shard_map/ppermute | solution.py:477
  103.2 7.8 %collective-permute-start.13 = (bf16[512,128]{1,0:T(8,128)(2,1)}, bf16[512,128]{1,0:T(8,128)(2,1)S(1)}, u32[]{:S(2)}, u32[]{:S(2)}) collective-permute-start(bf16[512,128]{1,0:T(8,128)(2,1)} %get-tuple-element.76), channel_id=1, source_target_pairs={{0,2},{2,4},{4,6},{6,0},{1,3},{3,5},{5,7},{7,1},{8,10},{10,12},{12... | collective-permute-start | bytes 393224 | tf_op jit(solution)/shard_map/ppermute | solution.py:477
  110.9 55.4 %copy-start = (s32[64]{0:T(128)S(1)}, s32[64]{0:T(128)}, u32[]{:S(2)}) copy-start(s32[64]{0:T(128)} %get-tuple-element.55.refs_0_.slot_of) | copy-start | bytes 772
  112.7 33.8 %collective-permute-start.16 = (bf16[4,512,128]{2,1,0:T(8,128)(2,1)}, bf16[4,512,128]{2,1,0:T(8,128)(2,1)}, u32[]{:S(2)}, u32[]{:S(2)}) collective-permute-start(bf16[4,512,128]{2,1,0:T(8,128)(2,1)} %pad_maximum_fusion.own), channel_id=1, source_target_pairs={{0,1},{1,0},{2,3},{3,2},{4,5},{5,4},{6,7},{7,6},{8,9},{9,8},{10,11... | collective-permute-start | bytes 1572872 | tf_op jit(solution)/shard_map/ppermute | solution.py:513
  114.2 9.2 %collective-permute-start.26 = (bf16[256,128]{1,0:T(8,128)(2,1)S(1)}, bf16[256,128]{1,0:T(8,128)(2,1)S(1)}, u32[]{:S(2)}, u32[]{:S(2)}) collective-permute-start(bf16[256,128]{1,0:T(8,128)(2,1)S(1)} %get-tuple-element.86.refs_0_), channel_id=1, source_target_pairs={{0,56},{8,0},{16,8},{24,16},{32,24},{40,32},{48,40},{56,48},{1,57}... | collective-permute-start | bytes 196616 | tf_op jit(solution)/shard_map/ppermute | solution.py:480
  116.8 6.6 %collective-permute-start.25 = (bf16[256,128]{1,0:T(8,128)(2,1)S(1)}, bf16[256,128]{1,0:T(8,128)(2,1)S(1)}, u32[]{:S(2)}, u32[]{:S(2)}) collective-permute-start(bf16[256,128]{1,0:T(8,128)(2,1)S(1)} %get-tuple-element.86.refs_0_), channel_id=1, source_target_pairs={{0,48},{8,56},{16,0},{24,8},{32,16},{40,24},{48,32},{56,40},{1,49}... | collective-permute-start | bytes 196616 | tf_op jit(solution)/shard_map/ppermute | solution.py:480
  118.9 7.7 %collective-permute-start.24 = (bf16[256,128]{1,0:T(8,128)(2,1)S(1)}, bf16[256,128]{1,0:T(8,128)(2,1)S(1)}, u32[]{:S(2)}, u32[]{:S(2)}) collective-permute-start(bf16[256,128]{1,0:T(8,128)(2,1)S(1)} %get-tuple-element.86.refs_0_), channel_id=1, source_target_pairs={{0,40},{8,48},{16,56},{24,0},{32,8},{40,16},{48,24},{56,32},{1,41}... | collective-permute-start | bytes 196616 | tf_op jit(solution)/shard_map/ppermute | solution.py:480
  120.1 7.8 %collective-permute-start.23 = (bf16[256,128]{1,0:T(8,128)(2,1)S(1)}, bf16[256,128]{1,0:T(8,128)(2,1)S(1)}, u32[]{:S(2)}, u32[]{:S(2)}) collective-permute-start(bf16[256,128]{1,0:T(8,128)(2,1)S(1)} %get-tuple-element.86.refs_0_), channel_id=1, source_target_pairs={{0,32},{8,40},{16,48},{24,56},{32,0},{40,8},{48,16},{56,24},{1,33}... | collective-permute-start | bytes 196616 | tf_op jit(solution)/shard_map/ppermute | solution.py:480
  123.4 9.6 %collective-permute-start.22 = (bf16[256,128]{1,0:T(8,128)(2,1)S(1)}, bf16[256,128]{1,0:T(8,128)(2,1)S(1)}, u32[]{:S(2)}, u32[]{:S(2)}) collective-permute-start(bf16[256,128]{1,0:T(8,128)(2,1)S(1)} %get-tuple-element.86.refs_0_), channel_id=1, source_target_pairs={{0,24},{8,32},{16,40},{24,48},{32,56},{40,0},{48,8},{56,16},{1,25}... | collective-permute-start | bytes 196616 | tf_op jit(solution)/shard_map/ppermute | solution.py:480
  123.4 12.3 %collective-permute-start.21 = (bf16[256,128]{1,0:T(8,128)(2,1)S(1)}, bf16[256,128]{1,0:T(8,128)(2,1)S(1)}, u32[]{:S(2)}, u32[]{:S(2)}) collective-permute-start(bf16[256,128]{1,0:T(8,128)(2,1)S(1)} %get-tuple-element.86.refs_0_), channel_id=1, source_target_pairs={{0,16},{8,24},{16,32},{24,40},{32,48},{40,56},{48,0},{56,8},{1,17}... | collective-permute-start | bytes 196616 | tf_op jit(solution)/shard_map/ppermute | solution.py:480
  126.7 9.8 %collective-permute-start.20 = (bf16[256,128]{1,0:T(8,128)(2,1)S(1)}, bf16[256,128]{1,0:T(8,128)(2,1)S(1)}, u32[]{:S(2)}, u32[]{:S(2)}) collective-permute-start(bf16[256,128]{1,0:T(8,128)(2,1)S(1)} %get-tuple-element.86.refs_0_), channel_id=1, source_target_pairs={{0,8},{8,16},{16,24},{24,32},{32,40},{40,48},{48,56},{56,0},{1,9},... | collective-permute-start | bytes 196616 | tf_op jit(solution)/shard_map/ppermute | solution.py:480
  137.8 6.9 %collective-permute-start.27 = (bf16[1024,128]{1,0:T(8,128)(2,1)S(1)}, bf16[1024,128]{1,0:T(8,128)(2,1)S(1)}, u32[]{:S(2)}, u32[]{:S(2)}) collective-permute-start(bf16[1024,128]{1,0:T(8,128)(2,1)S(1)} %get-tuple-element.88), channel_id=1, source_target_pairs={{0,192},{64,0},{128,64},{192,128},{1,193},{65,1},{129,65},{193,129... | collective-permute-start | bytes 786440 | tf_op jit(solution)/shard_map/ppermute | solution.py:480
  139.8 16.9 %collective-permute-start.28 = (bf16[1024,128]{1,0:T(8,128)(2,1)S(1)}, bf16[1024,128]{1,0:T(8,128)(2,1)S(1)}, u32[]{:S(2)}, u32[]{:S(2)}) collective-permute-start(bf16[1024,128]{1,0:T(8,128)(2,1)S(1)} %get-tuple-element.89), channel_id=1, source_target_pairs={{0,128},{64,192},{128,0},{192,64},{1,129},{65,193},{129,1},{193,65... | collective-permute-start | bytes 786440 | tf_op jit(solution)/shard_map/ppermute | solution.py:480
  140.7 16.3 %collective-permute-start.29 = (bf16[1024,128]{1,0:T(8,128)(2,1)S(1)}, bf16[1024,128]{1,0:T(8,128)(2,1)S(1)}, u32[]{:S(2)}, u32[]{:S(2)}) collective-permute-start(bf16[1024,128]{1,0:T(8,128)(2,1)S(1)} %get-tuple-element.90), channel_id=1, source_target_pairs={{0,64},{64,128},{128,192},{192,0},{1,65},{65,129},{129,193},{193,1... | collective-permute-start | bytes 786440 | tf_op jit(solution)/shard_map/ppermute | solution.py:480
  142.0 15.0 %collective-permute-start.17 = (bf16[1024,128]{1,0:T(8,128)(2,1)S(1)}, bf16[1024,128]{1,0:T(8,128)(2,1)S(1)}, u32[]{:S(2)}, u32[]{:S(2)}) collective-permute-start(bf16[1024,128]{1,0:T(8,128)(2,1)S(1)} %get-tuple-element.83), channel_id=1, source_target_pairs={{0,192},{64,0},{128,64},{192,128},{1,193},{65,1},{129,65},{193,129... | collective-permute-start | bytes 786440 | tf_op jit(solution)/shard_map/ppermute | solution.py:480
  144.7 13.5 %collective-permute-start.18 = (bf16[1024,128]{1,0:T(8,128)(2,1)S(1)}, bf16[1024,128]{1,0:T(8,128)(2,1)S(1)}, u32[]{:S(2)}, u32[]{:S(2)}) collective-permute-start(bf16[1024,128]{1,0:T(8,128)(2,1)S(1)} %get-tuple-element.84), channel_id=1, source_target_pairs={{0,128},{64,192},{128,0},{192,64},{1,129},{65,193},{129,1},{193,65... | collective-permute-start | bytes 786440 | tf_op jit(solution)/shard_map/ppermute | solution.py:480
  146.5 19.9 %collective-permute-start.19 = (bf16[1024,128]{1,0:T(8,128)(2,1)S(1)}, bf16[1024,128]{1,0:T(8,128)(2,1)S(1)}, u32[]{:S(2)}, u32[]{:S(2)}) collective-permute-start(bf16[1024,128]{1,0:T(8,128)(2,1)S(1)} %get-tuple-element.85), channel_id=1, source_target_pairs={{0,64},{64,128},{128,192},{192,0},{1,65},{65,129},{129,193},{193,1... | collective-permute-start | bytes 786440 | tf_op jit(solution)/shard_map/ppermute | solution.py:480
  167.5 2.2 %collective-permute-start.34 = (bf16[4,32,16,128]{3,2,1,0:T(8,128)(2,1)S(1)}, bf16[4,32,16,128]{3,2,1,0:T(8,128)(2,1)S(1)}, u32[]{:S(2)}, u32[]{:S(2)}) collective-permute-start(bf16[4,32,16,128]{3,2,1,0:T(8,128)(2,1)S(1)} %get-tuple-element.99), channel_id=1, source_target_pairs={{0,1},{1,0},{2,3},{3,2},{4,5},{5,4},{6,7},{7,6},{8,9},{9,8},{10,11... | collective-permute-start | bytes 1572872 | tf_op jit(solution)/shard_map/ppermute | solution.py:519
  169.2 3.9 %collective-permute-start.30 = (bf16[4,32,16,128]{3,2,1,0:T(8,128)(2,1)S(1)}, bf16[4,32,16,128]{3,2,1,0:T(8,128)(2,1)S(1)}, u32[]{:S(2)}, u32[]{:S(2)}) collective-permute-start(bf16[4,32,16,128]{3,2,1,0:T(8,128)(2,1)S(1)} %get-tuple-element.93), channel_id=1, source_target_pairs={{0,1},{1,0},{2,3},{3,2},{4,5},{5,4},{6,7},{7,6},{8,9},{9,8},{10,11... | collective-permute-start | bytes 1572872 | tf_op jit(solution)/shard_map/ppermute | solution.py:519
  169.8 8.3 %collective-permute-start.35 = (bf16[32,16,128]{2,1,0:T(8,128)(2,1)S(1)}, bf16[32,16,128]{2,1,0:T(8,128)(2,1)S(1)}, u32[]{:S(2)}, u32[]{:S(2)}) collective-permute-start(bf16[32,16,128]{2,1,0:T(8,128)(2,1)S(1)} %get-tuple-element.101), channel_id=1, source_target_pairs={{0,2},{2,4},{4,6},{6,0},{1,3},{3,5},{5,7},{7,1},{8,10},{10,12},{12... | collective-permute-start | bytes 393224 | tf_op jit(solution)/shard_map/ppermute | solution.py:477
  169.9 8.3 %collective-permute-start.36 = (bf16[32,16,128]{2,1,0:T(8,128)(2,1)S(1)}, bf16[32,16,128]{2,1,0:T(8,128)(2,1)S(1)}, u32[]{:S(2)}, u32[]{:S(2)}) collective-permute-start(bf16[32,16,128]{2,1,0:T(8,128)(2,1)S(1)} %get-tuple-element.102), channel_id=1, source_target_pairs={{0,4},{2,6},{4,0},{6,2},{1,5},{3,7},{5,1},{7,3},{8,12},{10,14},{12... | collective-permute-start | bytes 393224 | tf_op jit(solution)/shard_map/ppermute | solution.py:477
  171.4 8.1 %collective-permute-start.37 = (bf16[32,16,128]{2,1,0:T(8,128)(2,1)S(1)}, bf16[32,16,128]{2,1,0:T(8,128)(2,1)S(1)}, u32[]{:S(2)}, u32[]{:S(2)}) collective-permute-start(bf16[32,16,128]{2,1,0:T(8,128)(2,1)S(1)} %get-tuple-element.103), channel_id=1, source_target_pairs={{0,6},{2,0},{4,2},{6,4},{1,7},{3,1},{5,3},{7,5},{8,14},{10,8},{12,... | collective-permute-start | bytes 393224 | tf_op jit(solution)/shard_map/ppermute | solution.py:477
  173.3 11.0 %collective-permute-start.31 = (bf16[32,16,128]{2,1,0:T(8,128)(2,1)S(1)}, bf16[32,16,128]{2,1,0:T(8,128)(2,1)S(1)}, u32[]{:S(2)}, u32[]{:S(2)}) collective-permute-start(bf16[32,16,128]{2,1,0:T(8,128)(2,1)S(1)} %get-tuple-element.95), channel_id=1, source_target_pairs={{0,2},{2,4},{4,6},{6,0},{1,3},{3,5},{5,7},{7,1},{8,10},{10,12},{12... | collective-permute-start | bytes 393224 | tf_op jit(solution)/shard_map/ppermute | solution.py:477
  173.4 10.9 %collective-permute-start.32 = (bf16[32,16,128]{2,1,0:T(8,128)(2,1)S(1)}, bf16[32,16,128]{2,1,0:T(8,128)(2,1)S(1)}, u32[]{:S(2)}, u32[]{:S(2)}) collective-permute-start(bf16[32,16,128]{2,1,0:T(8,128)(2,1)S(1)} %get-tuple-element.96), channel_id=1, source_target_pairs={{0,4},{2,6},{4,0},{6,2},{1,5},{3,7},{5,1},{7,3},{8,12},{10,14},{12... | collective-permute-start | bytes 393224 | tf_op jit(solution)/shard_map/ppermute | solution.py:477
  178.2 6.3 %collective-permute-start.33 = (bf16[32,16,128]{2,1,0:T(8,128)(2,1)S(1)}, bf16[32,16,128]{2,1,0:T(8,128)(2,1)S(1)}, u32[]{:S(2)}, u32[]{:S(2)}) collective-permute-start(bf16[32,16,128]{2,1,0:T(8,128)(2,1)S(1)} %get-tuple-element.97), channel_id=1, source_target_pairs={{0,6},{2,0},{4,2},{6,4},{1,7},{3,1},{5,3},{7,5},{8,14},{10,8},{12,... | collective-permute-start | bytes 393224 | tf_op jit(solution)/shard_map/ppermute | solution.py:477
where the time goes:
time: 186 us; the launch traced here: 185 us
  starting transfers between devices  71.2 us (38%)
  waiting for transfers between devices  50.4 us (27%)
  Pallas kernels  37.8 us (20%)
  blocking collectives  21 us (11%)
  other arithmetic  3.12 us (2%)
    ppermute x26, starting transfers between devices, shift(): return lax.ppermute(value, name, [(i, (i + d) % n) for i in range(n)])  49.2 us
    ppermute x26, waiting for transfers between devices, shift(): return lax.ppermute(value, name, [(i, (i + d) % n) for i in range(n)])  34.4 us
    ppermute x9, waiting for transfers between devices, along_x(): lax.ppermute(value, 'x', [(i, (i + d) % x_count) for i in range(x_count)])  15.5 us
    all_to_all x1, blocking collectives, per_device(): sketch = lax.all_to_all(sketch, ROW, 0, 0, tiled=True)  12.5 us
    pallas_call x2, Pallas kernels, far_products(): pl.pallas_call(functools.partial(far_body, y_count, first), grid=(local /...  8.88 us
    all_to_all x1, blocking collectives, per_device(): basis_rows = lax.all_to_all(rows_sent, ROW, 0, 0, tiled=True)  8.48 us
    all_to_all x1, starting transfers between devices, per_device(): first = lax.all_to_all(dense, 'z', 0, 0, tiled=True)  8.2 us
    pallas_call x1, Pallas kernels, mixed_products(): pl.pallas_call(mixed_body, grid_spec=pltpu.PrefetchScalarGridSpec(num_sca...  7.7 us
  transfers between devices with their start and end apart: 40, of which 19 were waited for; matrix products, arithmetic and copies ran while one was open for 1% of the time, Pallas kernels for 12%

commit v1 on v0

--- a/solution.py
+++ b/solution.py
@@ -316,21 +316,23 @@
 
 
 def mixed_body(place, far, own, across, samples, mixed, parent, scratch):
-    j = pl.program_id(0)
-    far_count, rows, width = far.shape[1:]
+    step = pl.program_id(0)
+    pair, far_count, rows, width = far.shape
     cols = own.shape[2]
-    segment = jnp.where(j % 2 == place[0] % 2, own[0], across[0])
-    values = jnp.dot(far[0].reshape(far_count * rows, width), segment, preferred_element_type=F32)
-    mixed[pl.ds(j * far_count, far_count)] = values.astype(BF16).reshape(far_count, rows, cols)
-
-    @pl.when(j % 2 == place[0] // 4)
-    def _():
-        scratch[...] = lax.dot_general(
-            segment, samples[0], (((0,), (0,)), ((), ())), preferred_element_type=F32
-        ) / jnp.sqrt(F32(width))
-        count = parent.shape[1]
-        start = pl.multiple_of((place[0] % 4) * count, count)
-        parent[j // 2] = scratch[pl.ds(start, count)]
+    core, side = place[0] % 2, place[0] // 4
+    segments = [jnp.where(core == i, own[0], across[0]) for i in range(pair)]
+    for i in range(pair):
+        values = jnp.dot(far[i].reshape(far_count * rows, width), segments[i], preferred_element_type=F32)
+        start = pl.multiple_of((step * pair + i) * far_count, far_count)
+        mixed[pl.ds(start, far_count)] = values.astype(BF16).reshape(far_count, rows, cols)
+    scratch[...] = lax.dot_general(
+        jnp.where(side == 0, segments[0], segments[1]),
+        jnp.where(side == 0, samples[0], samples[1]),
+        (((0,), (0,)), ((), ())),
+        preferred_element_type=F32,
+    ) / jnp.sqrt(F32(width))
+    count = parent.shape[1]
+    parent[step] = scratch[pl.ds(pl.multiple_of((place[0] % 4) * count, count), count)]
 
 
 def mixed_products(place, far_kernel, own, across, samples):
@@ -338,18 +340,18 @@
     x_count, _, cols = own.shape
     parent_rows = 2 * cols // local
     side = pl.BlockSpec(
-        (1, width, cols), lambda j, place: ((place[0] // 2 + x_count - j // 2) % x_count, 0, 0)
+        (1, width, cols), lambda j, place: ((place[0] // 2 + x_count - j) % x_count, 0, 0)
     )
     return pl.pallas_call(
         mixed_body,
         grid_spec=pltpu.PrefetchScalarGridSpec(
             num_scalar_prefetch=1,
-            grid=(local,),
+            grid=(local // 2,),
             in_specs=[
-                pl.BlockSpec((1, far_count, rows, width), lambda j, *_: (j, 0, 0, 0)),
+                pl.BlockSpec((2, far_count, rows, width), lambda j, *_: (j, 0, 0, 0)),
                 side,
                 side,
-                pl.BlockSpec((1, width, cols), lambda j, *_: (j, 0, 0)),
+                pl.BlockSpec((2, width, cols), lambda j, *_: (j, 0, 0)),
             ],
             out_specs=[VMEM_SPEC, VMEM_SPEC],
             scratch_shapes=[pltpu.VMEM((cols, cols), F32)],

time: 186 us -> 186 us (level)
  waiting for transfers between devices: 50.4 us -> 53.1 us
  Pallas kernels: 37.8 us -> 35.2 us
    ppermute x26, waiting for transfers between devices: 34.4 us -> 37.1 us  [shift(): return lax.ppermute(value, name, [(i, (i + d) % n) for i in range(n)])]
    pallas_call x1, Pallas kernels: 7.7 us -> 5 us  [mixed_products(): pl.pallas_call(mixed_body, grid_spec=pltpu.PrefetchScalarGridSpec(num_sca...]
  transfers between devices with their start and end apart: 40 -> 40, of which waited for: 19 -> 19; matrix products, arithmetic and copies ran while one was open for 1% -> 1% of each run, Pallas kernels for 12% -> 10%
where the time goes in v1:
time: 186 us; the launch traced here: 185 us
  starting transfers between devices  71.2 us (38%)
  waiting for transfers between devices  53.1 us (29%)
  Pallas kernels  35.2 us (19%)
  blocking collectives  21 us (11%)
  other arithmetic  3.12 us (2%)
    ppermute x26, starting transfers between devices, shift(): return lax.ppermute(value, name, [(i, (i + d) % n) for i in range(n)])  49.2 us
    ppermute x26, waiting for transfers between devices, shift(): return lax.ppermute(value, name, [(i, (i + d) % n) for i in range(n)])  37.1 us
    ppermute x9, waiting for transfers between devices, along_x(): lax.ppermute(value, 'x', [(i, (i + d) % x_count) for i in range(x_count)])  15.5 us
    all_to_all x1, blocking collectives, per_device(): sketch = lax.all_to_all(sketch, ROW, 0, 0, tiled=True)  12.5 us
    pallas_call x2, Pallas kernels, far_products(): pl.pallas_call(functools.partial(far_body, y_count, first), grid=(local /...  8.88 us
    all_to_all x1, blocking collectives, per_device(): basis_rows = lax.all_to_all(rows_sent, ROW, 0, 0, tiled=True)  8.48 us
    all_to_all x1, starting transfers between devices, per_device(): first = lax.all_to_all(dense, 'z', 0, 0, tiled=True)  8.2 us
    ppermute x9, starting transfers between devices, along_x(): lax.ppermute(value, 'x', [(i, (i + d) % x_count) for i in range(x_count)])  7.36 us
  transfers between devices with their start and end apart: 40, of which 19 were waited for; matrix products, arithmetic and copies ran while one was open for 1% of the time, Pallas kernels for 10%

profile of v1, /device:TPU:1, one launch (start us, length us, event | category | flops | bytes accessed | tf_op | source)
XLA Modules:
  0.0 185.3 jit_solution(15415399797344437040)
XLA Ops:
  0.6 4.8 %shard_map.67 = (bf16[1024,128]{1,0:T(8,128)(2,1)S(1)}, bf16[1032,128]{1,0:T(8,128)(2,1)}, bf16[1032,128]{1,0:T(8,128)(2,1)S(1)}, bf16[1032,128]{1,0:T(8,128)(2,1)S(1)}, s32[64]{0:T(128)}, /*index=5*/s32[128]{0:T(128)}) custom-call(s32[1]{0:T(128)} %bitcast.refs_0_, s32[8,8]{1,0:T(8,128)} %refs_1_.2, bf16[8,8,64,512]{3,2,1,0:T(8,128)(2,1)} %far.1, ...), custom_call_target="tpu_custom_call" | custom-call | flops 268435456 | bytes 4000000 | tf_op jit(solution)/shard_map/pallas_call | solution.py:100
  5.4 2.2 %collective-permute-start = (bf16[1032,128]{1,0:T(8,128)(2,1)}, bf16[1032,128]{1,0:T(8,128)(2,1)S(1)}, u32[]{:S(2)}, u32[]{:S(2)}) collective-permute-start(bf16[1032,128]{1,0:T(8,128)(2,1)} %get-tuple-element.59), channel_id=1, source_target_pairs={{0,64},{64,128},{128,192},{192,0},{1,65},{65,129},{129,193},{193,1... | collective-permute-start | bytes 792584 | tf_op jit(solution)/shard_map/ppermute | solution.py:482
  7.6 2.6 %collective-permute-start.1 = (bf16[1032,128]{1,0:T(8,128)(2,1)S(1)}, bf16[1032,128]{1,0:T(8,128)(2,1)S(1)}, u32[]{:S(2)}, u32[]{:S(2)}) collective-permute-start(bf16[1032,128]{1,0:T(8,128)(2,1)S(1)} %get-tuple-element.60), channel_id=1, source_target_pairs={{0,128},{64,192},{128,0},{192,64},{1,129},{65,193},{129,1},{193,65... | collective-permute-start | bytes 792584 | tf_op jit(solution)/shard_map/ppermute | solution.py:482
  10.2 1.1 collective-permute-start.2
  11.3 3.8 %near_products.1.refs_8_ = f32[8,64,128]{2,1,0:T(8,128)} custom-call(bf16[8,2,64,512]{3,2,1,0:T(8,128)(2,1)} %near.1, bf16[8,512,128]{2,1,0:T(8,128)(2,1)} %samples.3), custom_call_target="tpu_custom_call" | custom-call | flops 134217728 | bytes 2500000 | tf_op jit(solution)/shard_map/near_products/pallas_call | solution.py:128
  15.1 4.1 %shard_map.68 = (bf16[1024,128]{1,0:T(8,128)(2,1)S(1)}, bf16[1024,128]{1,0:T(8,128)(2,1)}, bf16[1024,128]{1,0:T(8,128)(2,1)}, bf16[1024,128]{1,0:T(8,128)(2,1)S(1)}, s32[1]{0:T(128)}) custom-call(s32[64]{0:T(128)} %get-tuple-element.55.refs_0_.slot_of, bf16[8,8,64,512]{3,2,1,0:T(8,128)(2,1)} %far.1, bf16[8,512,128]{2,1,0:T(8,128)(2,1)} %samples.3), custom_call_target="tpu_custom_call" | custom-call | flops 268435456 | bytes 4000000 | tf_op jit(solution)/shard_map/pallas_call | solution.py:100
  20.0 1.8 collective-permute-done.1.refs_2_
  22.7 2.3 %shard_map.69 = bf16[8,256,128]{2,1,0:T(8,128)(2,1)} custom-call(s32[4,8,4]{2,1,0:T(8,128)} %pad_add_fusion.ids, s32[1]{0:T(128)} %bitcast.5.place, bf16[1024,128]{1,0:T(8,128)(2,1)S(1)} %get-tuple-element.62.refs_0_, bf16[1032,128]{1,0:T(8,128)(2,1)S(1)} %collective-permute-done.refs_1_, bf16[1032,128]{1,0:T(8,128)(2,1)S(1)} %collective-permute-done.1.refs_2_, ...), custom_call_target="tpu_custom_call" | custom-call | flops 1000000 | bytes 1600000 | tf_op jit(solution)/shard_map/pallas_call | solution.py:175
  25.0 8.2 %all-to-all-start = ((bf16[8,256,128]{2,1,0:T(8,128)(2,1)}), bf16[8,256,128]{2,1,0:T(8,128)(2,1)S(1)}, u32[]{:S(2)}, u32[]{:S(2)}) async-start(bf16[8,256,128]{2,1,0:T(8,128)(2,1)} %shard_map.69), calls=%async_computation | async-start | bytes 1048576 | tf_op jit(solution)/shard_map/all_to_all | solution.py:497
  33.2 1.0 collective-permute-start.3
  34.2 2.8 %collective-permute-start.4 = (bf16[1024,128]{1,0:T(8,128)(2,1)}, bf16[1024,128]{1,0:T(8,128)(2,1)S(1)}, u32[]{:S(2)}, u32[]{:S(2)}) collective-permute-start(bf16[1024,128]{1,0:T(8,128)(2,1)} %get-tuple-element.65), channel_id=1, source_target_pairs={{0,128},{64,192},{128,0},{192,64},{1,129},{65,193},{129,1},{193,65... | collective-permute-start | bytes 786440 | tf_op jit(solution)/shard_map/ppermute | solution.py:482
  37.0 3.7 %collective-permute-done.3.refs_1_ = bf16[1024,128]{1,0:T(8,128)(2,1)S(1)} collective-permute-done((bf16[1024,128]{1,0:T(8,128)(2,1)}, bf16[1024,128]{1,0:T(8,128)(2,1)S(1)}, u32[]{:S(2)}, u32[]{:S(2)}) %collective-permute-start.3) | collective-permute-done | bytes 262176 | tf_op jit(solution)/shard_map/ppermute | solution.py:482
  40.6 7.8 %collective-permute-done.4.refs_2_ = bf16[1024,128]{1,0:T(8,128)(2,1)S(1)} collective-permute-done((bf16[1024,128]{1,0:T(8,128)(2,1)}, bf16[1024,128]{1,0:T(8,128)(2,1)S(1)}, u32[]{:S(2)}, u32[]{:S(2)}) %collective-permute-start.4) | collective-permute-done | bytes 262176 | tf_op jit(solution)/shard_map/ppermute | solution.py:482
  48.4 1.5 shard_map.70
  49.9 5.2 %collective-permute-start.6 = (bf16[256,128]{1,0:T(8,128)(2,1)S(1)}, bf16[256,128]{1,0:T(8,128)(2,1)S(1)}, u32[]{:S(2)}, u32[]{:S(2)}) collective-permute-start(bf16[256,128]{1,0:T(8,128)(2,1)S(1)} %get-tuple-element.68), channel_id=1, source_target_pairs={{0,32},{8,40},{16,48},{24,56},{32,0},{40,8},{48,16},{56,24},{1,33}... | collective-permute-start | bytes 196616 | tf_op jit(solution)/shard_map/ppermute | solution.py:482
  55.4 4.2 %collective-permute-start.8 = (bf16[256,128]{1,0:T(8,128)(2,1)S(1)}, bf16[256,128]{1,0:T(8,128)(2,1)S(1)}, u32[]{:S(2)}, u32[]{:S(2)}) collective-permute-start(bf16[256,128]{1,0:T(8,128)(2,1)S(1)} %get-tuple-element.70), channel_id=1, source_target_pairs={{0,40},{8,48},{16,56},{24,0},{32,8},{40,16},{48,24},{56,32},{1,41}... | collective-permute-start | bytes 196616 | tf_op jit(solution)/shard_map/ppermute | solution.py:482
  59.9 3.3 %collective-permute-start.10 = (bf16[256,128]{1,0:T(8,128)(2,1)S(1)}, bf16[256,128]{1,0:T(8,128)(2,1)S(1)}, u32[]{:S(2)}, u32[]{:S(2)}) collective-permute-start(bf16[256,128]{1,0:T(8,128)(2,1)S(1)} %get-tuple-element.72), channel_id=1, source_target_pairs={{0,48},{8,56},{16,0},{24,8},{32,16},{40,24},{48,32},{56,40},{1,49}... | collective-permute-start | bytes 196616 | tf_op jit(solution)/shard_map/ppermute | solution.py:482
  63.4 2.4 %collective-permute-start.12 = (bf16[256,128]{1,0:T(8,128)(2,1)S(1)}, bf16[256,128]{1,0:T(8,128)(2,1)S(1)}, u32[]{:S(2)}, u32[]{:S(2)}) collective-permute-start(bf16[256,128]{1,0:T(8,128)(2,1)S(1)} %get-tuple-element.74), channel_id=1, source_target_pairs={{0,56},{8,0},{16,8},{24,16},{32,24},{40,32},{48,40},{56,48},{1,57}... | collective-permute-start | bytes 196616 | tf_op jit(solution)/shard_map/ppermute | solution.py:482
  65.8 0.7 collective-permute-done.10.refs_5_
  66.6 2.2 %collective-permute-done.11.refs_6_ = bf16[256,128]{1,0:T(8,128)(2,1)S(1)} collective-permute-done((bf16[256,128]{1,0:T(8,128)(2,1)S(1)}, bf16[256,128]{1,0:T(8,128)(2,1)S(1)}, u32[]{:S(2)}, u32[]{:S(2)}) %collective-permute-start.11) | collective-permute-done | bytes 65568 | tf_op jit(solution)/shard_map/ppermute | solution.py:482
  68.8 1.1 dense_sum.1
  69.9 12.5 %all_to_all.20.sketch = bf16[8,64,128]{2,1,0:T(8,128)(2,1)S(1)} all-to-all(bf16[8,64,128]{2,1,0:T(8,128)(2,1)S(1)} %dense_sum.1), channel_id=1, replica_groups=mesh['y'=4,'z'=8,'x'=4,'core'=2] {'x','core'}, dimensions={0} | all-to-all | bytes 262144 | tf_op jit(solution)/shard_map/all_to_all | solution.py:502
  82.4 5.1 %basis_of.1 = (bf16[8,64,128]{2,1,0:T(8,128)(2,1)S(1)}, bf16[512,128]{1,0:T(8,128)(2,1)}) custom-call(bf16[8,64,128]{2,1,0:T(8,128)(2,1)S(1)} %all_to_all.20.sketch), custom_call_target="tpu_custom_call" | custom-call | flops 500000000 | bytes 1000000 | tf_op jit(solution)/shard_map/basis_of/pallas_call | solution.py:259
  87.5 8.5 %all_to_all.21.basis = bf16[8,64,128]{2,1,0:T(8,128)(2,1)S(1)} all-to-all(bf16[8,64,128]{2,1,0:T(8,128)(2,1)S(1)} %get-tuple-element.77), channel_id=1, replica_groups=mesh['y'=4,'z'=8,'x'=4,'core'=2] {'x','core'}, dimensions={0} | all-to-all | bytes 262144 | tf_op jit(solution)/shard_map/all_to_all | solution.py:504
  96.0 0.9 spread.1
  96.9 4.2 %all-to-all-start.3 = ((bf16[8,256,128]{2,1,0:T(8,128)(2,1)}), bf16[8,256,128]{2,1,0:T(8,128)(2,1)S(1)}, u32[]{:S(2)}, u32[]{:S(2)}) async-start(bf16[8,256,128]{2,1,0:T(8,128)(2,1)} %get-tuple-element.81), calls=%async_computation.3 | async-start | bytes 1048576 | tf_op jit(solution)/shard_map/all_to_all | solution.py:506
  101.1 0.9 collective-permute-start.15
  102.0 1.2 collective-permute-start.14
  103.2 0.7 convert_element_type.7
  103.9 1.2 collective-permute-done.15
  105.1 2.4 %collective-permute-done.14 = bf16[512,128]{1,0:T(8,128)(2,1)S(1)} collective-permute-done((bf16[512,128]{1,0:T(8,128)(2,1)}, bf16[512,128]{1,0:T(8,128)(2,1)S(1)}, u32[]{:S(2)}, u32[]{:S(2)}) %collective-permute-start.14) | collective-permute-done | bytes 131104 | tf_op jit(solution)/shard_map/ppermute | solution.py:479
  107.5 3.4 %collective-permute-done.13 = bf16[512,128]{1,0:T(8,128)(2,1)S(1)} collective-permute-done((bf16[512,128]{1,0:T(8,128)(2,1)}, bf16[512,128]{1,0:T(8,128)(2,1)S(1)}, u32[]{:S(2)}, u32[]{:S(2)}) %collective-permute-start.13) | collective-permute-done | bytes 131104 | tf_op jit(solution)/shard_map/ppermute | solution.py:479
  110.9 1.8 pad_maximum_fusion.own
  112.7 1.5 collective-permute-start.16
  114.2 2.7 %collective-permute-start.26 = (bf16[256,128]{1,0:T(8,128)(2,1)S(1)}, bf16[256,128]{1,0:T(8,128)(2,1)S(1)}, u32[]{:S(2)}, u32[]{:S(2)}) collective-permute-start(bf16[256,128]{1,0:T(8,128)(2,1)S(1)} %get-tuple-element.86.refs_0_), channel_id=1, source_target_pairs={{0,56},{8,0},{16,8},{24,16},{32,24},{40,32},{48,40},{56,48},{1,57}... | collective-permute-start | bytes 196616 | tf_op jit(solution)/shard_map/ppermute | solution.py:482
  116.8 2.1 %collective-permute-start.25 = (bf16[256,128]{1,0:T(8,128)(2,1)S(1)}, bf16[256,128]{1,0:T(8,128)(2,1)S(1)}, u32[]{:S(2)}, u32[]{:S(2)}) collective-permute-start(bf16[256,128]{1,0:T(8,128)(2,1)S(1)} %get-tuple-element.86.refs_0_), channel_id=1, source_target_pairs={{0,48},{8,56},{16,0},{24,8},{32,16},{40,24},{48,32},{56,40},{1,49}... | collective-permute-start | bytes 196616 | tf_op jit(solution)/shard_map/ppermute | solution.py:482
  118.9 1.2 collective-permute-start.24
  120.1 3.3 %collective-permute-start.23 = (bf16[256,128]{1,0:T(8,128)(2,1)S(1)}, bf16[256,128]{1,0:T(8,128)(2,1)S(1)}, u32[]{:S(2)}, u32[]{:S(2)}) collective-permute-start(bf16[256,128]{1,0:T(8,128)(2,1)S(1)} %get-tuple-element.86.refs_0_), channel_id=1, source_target_pairs={{0,32},{8,40},{16,48},{24,56},{32,0},{40,8},{48,16},{56,24},{1,33}... | collective-permute-start | bytes 196616 | tf_op jit(solution)/shard_map/ppermute | solution.py:482
  123.4 3.3 %collective-permute-start.21 = (bf16[256,128]{1,0:T(8,128)(2,1)S(1)}, bf16[256,128]{1,0:T(8,128)(2,1)S(1)}, u32[]{:S(2)}, u32[]{:S(2)}) collective-permute-start(bf16[256,128]{1,0:T(8,128)(2,1)S(1)} %get-tuple-element.86.refs_0_), channel_id=1, source_target_pairs={{0,16},{8,24},{16,32},{24,40},{32,48},{40,56},{48,0},{56,8},{1,17}... | collective-permute-start | bytes 196616 | tf_op jit(solution)/shard_map/ppermute | solution.py:482
  126.7 1.2 collective-permute-start.20
  127.9 5.1 %collective-permute-done.22.refs_3_ = bf16[256,128]{1,0:T(8,128)(2,1)S(1)} collective-permute-done((bf16[256,128]{1,0:T(8,128)(2,1)S(1)}, bf16[256,128]{1,0:T(8,128)(2,1)S(1)}, u32[]{:S(2)}, u32[]{:S(2)}) %collective-permute-start.22) | collective-permute-done | bytes 65568 | tf_op jit(solution)/shard_map/ppermute | solution.py:482
  133.0 2.7 %collective-permute-done.21.refs_2_ = bf16[256,128]{1,0:T(8,128)(2,1)S(1)} collective-permute-done((bf16[256,128]{1,0:T(8,128)(2,1)S(1)}, bf16[256,128]{1,0:T(8,128)(2,1)S(1)}, u32[]{:S(2)}, u32[]{:S(2)}) %collective-permute-start.21) | collective-permute-done | bytes 65568 | tf_op jit(solution)/shard_map/ppermute | solution.py:482
  135.7 0.8 collective-permute-done.20.refs_1_
  136.4 1.4 shard_map.72
  137.8 2.0 %collective-permute-start.27 = (bf16[1024,128]{1,0:T(8,128)(2,1)S(1)}, bf16[1024,128]{1,0:T(8,128)(2,1)S(1)}, u32[]{:S(2)}, u32[]{:S(2)}) collective-permute-start(bf16[1024,128]{1,0:T(8,128)(2,1)S(1)} %get-tuple-element.88), channel_id=1, source_target_pairs={{0,192},{64,0},{128,64},{192,128},{1,193},{65,1},{129,65},{193,129... | collective-permute-start | bytes 786440 | tf_op jit(solution)/shard_map/ppermute | solution.py:482
  139.8 0.9 collective-permute-start.28
  140.7 1.3 shard_map.71
  142.0 2.8 %collective-permute-start.17 = (bf16[1024,128]{1,0:T(8,128)(2,1)S(1)}, bf16[1024,128]{1,0:T(8,128)(2,1)S(1)}, u32[]{:S(2)}, u32[]{:S(2)}) collective-permute-start(bf16[1024,128]{1,0:T(8,128)(2,1)S(1)} %get-tuple-element.83), channel_id=1, source_target_pairs={{0,192},{64,0},{128,64},{192,128},{1,193},{65,1},{129,65},{193,129... | collective-permute-start | bytes 786440 | tf_op jit(solution)/shard_map/ppermute | solution.py:482
  144.7 1.8 collective-permute-start.18
  146.5 2.5 %collective-permute-start.19 = (bf16[1024,128]{1,0:T(8,128)(2,1)S(1)}, bf16[1024,128]{1,0:T(8,128)(2,1)S(1)}, u32[]{:S(2)}, u32[]{:S(2)}) collective-permute-start(bf16[1024,128]{1,0:T(8,128)(2,1)S(1)} %get-tuple-element.85), channel_id=1, source_target_pairs={{0,64},{64,128},{128,192},{192,0},{1,65},{65,129},{129,193},{193,1... | collective-permute-start | bytes 786440 | tf_op jit(solution)/shard_map/ppermute | solution.py:482
  149.0 5.0 %mixed_products.1 = (bf16[64,64,128]{2,1,0:T(8,128)(2,1)S(1)}, f32[4,32,128]{2,1,0:T(8,128)}) custom-call(s32[1]{0:T(128)} %bitcast.10.place, bf16[8,8,64,512]{3,2,1,0:T(8,128)(2,1)} %far.1, bf16[4,512,128]{2,1,0:T(8,128)(2,1)} %pad_maximum_fusion.own, bf16[4,512,128]{2,1,0:T(8,128)(2,1)} %collective-permute-done.16.across, bf16[8,512,128]{2,1,0:T(8,128)(2,1)} %samples.3), custom_call_target="tpu_custom_call" | custom-call | flops 536870912 | bytes 8000000 | tf_op jit(solution)/shard_map/mixed_products/pallas_call | solution.py:345
  154.0 3.0 %collective-permute-done.29.refs_7_ = bf16[1024,128]{1,0:T(8,128)(2,1)S(1)} collective-permute-done((bf16[1024,128]{1,0:T(8,128)(2,1)S(1)}, bf16[1024,128]{1,0:T(8,128)(2,1)S(1)}, u32[]{:S(2)}, u32[]{:S(2)}) %collective-permute-start.29) | collective-permute-done | bytes 262176 | tf_op jit(solution)/shard_map/ppermute | solution.py:482
  157.0 1.2 collective-permute-done.18.refs_2_
  158.2 8.2 %collective-permute-done.19.refs_3_ = bf16[1024,128]{1,0:T(8,128)(2,1)S(1)} collective-permute-done((bf16[1024,128]{1,0:T(8,128)(2,1)S(1)}, bf16[1024,128]{1,0:T(8,128)(2,1)S(1)}, u32[]{:S(2)}, u32[]{:S(2)}) %collective-permute-start.19) | collective-permute-done | bytes 262176 | tf_op jit(solution)/shard_map/ppermute | solution.py:482
  166.4 1.1 shard_map.73
  168.2 1.1 shard_map.74
  169.9 1.4 collective-permute-start.36
  171.4 1.8 collective-permute-start.37
  173.4 1.9 %collective-permute-start.32 = (bf16[32,16,128]{2,1,0:T(8,128)(2,1)S(1)}, bf16[32,16,128]{2,1,0:T(8,128)(2,1)S(1)}, u32[]{:S(2)}, u32[]{:S(2)}) collective-permute-start(bf16[32,16,128]{2,1,0:T(8,128)(2,1)S(1)} %get-tuple-element.96), channel_id=1, source_target_pairs={{0,4},{2,6},{4,0},{6,2},{1,5},{3,7},{5,1},{7,3},{8,12},{10,14},{12... | collective-permute-start | bytes 393224 | tf_op jit(solution)/shard_map/ppermute | solution.py:479
  175.2 2.9 %collective-permute-done.35.refs_1_ = bf16[32,16,128]{2,1,0:T(8,128)(2,1)S(1)} collective-permute-done((bf16[32,16,128]{2,1,0:T(8,128)(2,1)S(1)}, bf16[32,16,128]{2,1,0:T(8,128)(2,1)S(1)}, u32[]{:S(2)}, u32[]{:S(2)}) %collective-permute-start.35) | collective-permute-done | bytes 131104 | tf_op jit(solution)/shard_map/ppermute | solution.py:479
  178.2 1.2 collective-permute-done.37.refs_3_
  179.4 0.8 shard_map.77.refs_4_
  180.2 4.1 %collective-permute-done.31.refs_1_ = bf16[32,16,128]{2,1,0:T(8,128)(2,1)S(1)} collective-permute-done((bf16[32,16,128]{2,1,0:T(8,128)(2,1)S(1)}, bf16[32,16,128]{2,1,0:T(8,128)(2,1)S(1)}, u32[]{:S(2)}, u32[]{:S(2)}) %collective-permute-start.31) | collective-permute-done | bytes 131104 | tf_op jit(solution)/shard_map/ppermute | solution.py:479
  184.5 0.8 shard_map.78
  (48 shorter events, 3.7 us)
Async XLA Ops:
  5.4 14.4 %copy-start.1 = (s32[128]{0:T(128)S(1)}, s32[128]{0:T(128)}, u32[]{:S(2)}) copy-start(s32[128]{0:T(128)} %get-tuple-element.58) | copy-start | bytes 1540
  5.4 14.5 %collective-permute-start = (bf16[1032,128]{1,0:T(8,128)(2,1)}, bf16[1032,128]{1,0:T(8,128)(2,1)S(1)}, u32[]{:S(2)}, u32[]{:S(2)}) collective-permute-start(bf16[1032,128]{1,0:T(8,128)(2,1)} %get-tuple-element.59), channel_id=1, source_target_pairs={{0,64},{64,128},{128,192},{192,0},{1,65},{65,129},{129,193},{193,1... | collective-permute-start | bytes 792584 | tf_op jit(solution)/shard_map/ppermute | solution.py:482
  7.6 14.2 %collective-permute-start.1 = (bf16[1032,128]{1,0:T(8,128)(2,1)S(1)}, bf16[1032,128]{1,0:T(8,128)(2,1)S(1)}, u32[]{:S(2)}, u32[]{:S(2)}) collective-permute-start(bf16[1032,128]{1,0:T(8,128)(2,1)S(1)} %get-tuple-element.60), channel_id=1, source_target_pairs={{0,128},{64,192},{128,0},{192,64},{1,129},{65,193},{129,1},{193,65... | collective-permute-start | bytes 792584 | tf_op jit(solution)/shard_map/ppermute | solution.py:482
  10.2 11.7 %collective-permute-start.2 = (bf16[1032,128]{1,0:T(8,128)(2,1)S(1)}, bf16[1032,128]{1,0:T(8,128)(2,1)S(1)}, u32[]{:S(2)}, u32[]{:S(2)}) collective-permute-start(bf16[1032,128]{1,0:T(8,128)(2,1)S(1)} %get-tuple-element.61), channel_id=1, source_target_pairs={{0,192},{64,0},{128,64},{192,128},{1,193},{65,1},{129,65},{193,129... | collective-permute-start | bytes 792584 | tf_op jit(solution)/shard_map/ppermute | solution.py:482
  25.0 43.8 %all-to-all-start = ((bf16[8,256,128]{2,1,0:T(8,128)(2,1)}), bf16[8,256,128]{2,1,0:T(8,128)(2,1)S(1)}, u32[]{:S(2)}, u32[]{:S(2)}) async-start(bf16[8,256,128]{2,1,0:T(8,128)(2,1)} %shard_map.69), calls=%async_computation | async-start | bytes 1048576 | tf_op jit(solution)/shard_map/all_to_all | solution.py:497
  33.2 7.5 %collective-permute-start.3 = (bf16[1024,128]{1,0:T(8,128)(2,1)}, bf16[1024,128]{1,0:T(8,128)(2,1)S(1)}, u32[]{:S(2)}, u32[]{:S(2)}) collective-permute-start(bf16[1024,128]{1,0:T(8,128)(2,1)} %get-tuple-element.64), channel_id=1, source_target_pairs={{0,64},{64,128},{128,192},{192,0},{1,65},{65,129},{129,193},{193,1... | collective-permute-start | bytes 786440 | tf_op jit(solution)/shard_map/ppermute | solution.py:482
  34.2 14.2 %collective-permute-start.4 = (bf16[1024,128]{1,0:T(8,128)(2,1)}, bf16[1024,128]{1,0:T(8,128)(2,1)S(1)}, u32[]{:S(2)}, u32[]{:S(2)}) collective-permute-start(bf16[1024,128]{1,0:T(8,128)(2,1)} %get-tuple-element.65), channel_id=1, source_target_pairs={{0,128},{64,192},{128,0},{192,64},{1,129},{65,193},{129,1},{193,65... | collective-permute-start | bytes 786440 | tf_op jit(solution)/shard_map/ppermute | solution.py:482
  37.0 11.5 %collective-permute-start.5 = (bf16[1024,128]{1,0:T(8,128)(2,1)S(1)}, bf16[1024,128]{1,0:T(8,128)(2,1)S(1)}, u32[]{:S(2)}, u32[]{:S(2)}) collective-permute-start(bf16[1024,128]{1,0:T(8,128)(2,1)S(1)} %get-tuple-element.66), channel_id=1, source_target_pairs={{0,192},{64,0},{128,64},{192,128},{1,193},{65,1},{129,65},{193,129... | collective-permute-start | bytes 786440 | tf_op jit(solution)/shard_map/ppermute | solution.py:482
  49.9 13.2 %collective-permute-start.6 = (bf16[256,128]{1,0:T(8,128)(2,1)S(1)}, bf16[256,128]{1,0:T(8,128)(2,1)S(1)}, u32[]{:S(2)}, u32[]{:S(2)}) collective-permute-start(bf16[256,128]{1,0:T(8,128)(2,1)S(1)} %get-tuple-element.68), channel_id=1, source_target_pairs={{0,32},{8,40},{16,48},{24,56},{32,0},{40,8},{48,16},{56,24},{1,33}... | collective-permute-start | bytes 196616 | tf_op jit(solution)/shard_map/ppermute | solution.py:482
  55.1 8.3 %collective-permute-start.7 = (bf16[256,128]{1,0:T(8,128)(2,1)S(1)}, bf16[256,128]{1,0:T(8,128)(2,1)S(1)}, u32[]{:S(2)}, u32[]{:S(2)}) collective-permute-start(bf16[256,128]{1,0:T(8,128)(2,1)S(1)} %get-tuple-element.69), channel_id=1, source_target_pairs={{0,24},{8,32},{16,40},{24,48},{32,56},{40,0},{48,8},{56,16},{1,25}... | collective-permute-start | bytes 196616 | tf_op jit(solution)/shard_map/ppermute | solution.py:482
  55.4 10.5 %collective-permute-start.8 = (bf16[256,128]{1,0:T(8,128)(2,1)S(1)}, bf16[256,128]{1,0:T(8,128)(2,1)S(1)}, u32[]{:S(2)}, u32[]{:S(2)}) collective-permute-start(bf16[256,128]{1,0:T(8,128)(2,1)S(1)} %get-tuple-element.70), channel_id=1, source_target_pairs={{0,40},{8,48},{16,56},{24,0},{32,8},{40,16},{48,24},{56,32},{1,41}... | collective-permute-start | bytes 196616 | tf_op jit(solution)/shard_map/ppermute | solution.py:482
  59.6 6.3 %collective-permute-start.9 = (bf16[256,128]{1,0:T(8,128)(2,1)S(1)}, bf16[256,128]{1,0:T(8,128)(2,1)S(1)}, u32[]{:S(2)}, u32[]{:S(2)}) collective-permute-start(bf16[256,128]{1,0:T(8,128)(2,1)S(1)} %get-tuple-element.71), channel_id=1, source_target_pairs={{0,16},{8,24},{16,32},{24,40},{32,48},{40,56},{48,0},{56,8},{1,17}... | collective-permute-start | bytes 196616 | tf_op jit(solution)/shard_map/ppermute | solution.py:482
  59.9 6.7 %collective-permute-start.10 = (bf16[256,128]{1,0:T(8,128)(2,1)S(1)}, bf16[256,128]{1,0:T(8,128)(2,1)S(1)}, u32[]{:S(2)}, u32[]{:S(2)}) collective-permute-start(bf16[256,128]{1,0:T(8,128)(2,1)S(1)} %get-tuple-element.72), channel_id=1, source_target_pairs={{0,48},{8,56},{16,0},{24,8},{32,16},{40,24},{48,32},{56,40},{1,49}... | collective-permute-start | bytes 196616 | tf_op jit(solution)/shard_map/ppermute | solution.py:482
  63.2 5.6 %collective-permute-start.11 = (bf16[256,128]{1,0:T(8,128)(2,1)S(1)}, bf16[256,128]{1,0:T(8,128)(2,1)S(1)}, u32[]{:S(2)}, u32[]{:S(2)}) collective-permute-start(bf16[256,128]{1,0:T(8,128)(2,1)S(1)} %get-tuple-element.73), channel_id=1, source_target_pairs={{0,8},{8,16},{16,24},{24,32},{32,40},{40,48},{48,56},{56,0},{1,9},... | collective-permute-start | bytes 196616 | tf_op jit(solution)/shard_map/ppermute | solution.py:482
  63.4 5.3 %collective-permute-start.12 = (bf16[256,128]{1,0:T(8,128)(2,1)S(1)}, bf16[256,128]{1,0:T(8,128)(2,1)S(1)}, u32[]{:S(2)}, u32[]{:S(2)}) collective-permute-start(bf16[256,128]{1,0:T(8,128)(2,1)S(1)} %get-tuple-element.74), channel_id=1, source_target_pairs={{0,56},{8,0},{16,8},{24,16},{32,24},{40,32},{48,40},{56,48},{1,57}... | collective-permute-start | bytes 196616 | tf_op jit(solution)/shard_map/ppermute | solution.py:482
  96.9 43.8 %all-to-all-start.3 = ((bf16[8,256,128]{2,1,0:T(8,128)(2,1)}), bf16[8,256,128]{2,1,0:T(8,128)(2,1)S(1)}, u32[]{:S(2)}, u32[]{:S(2)}) async-start(bf16[8,256,128]{2,1,0:T(8,128)(2,1)} %get-tuple-element.81), calls=%async_computation.3 | async-start | bytes 1048576 | tf_op jit(solution)/shard_map/all_to_all | solution.py:506
  101.1 4.0 %collective-permute-start.15 = (bf16[512,128]{1,0:T(8,128)(2,1)}, bf16[512,128]{1,0:T(8,128)(2,1)S(1)}, u32[]{:S(2)}, u32[]{:S(2)}) collective-permute-start(bf16[512,128]{1,0:T(8,128)(2,1)} %get-tuple-element.76), channel_id=1, source_target_pairs={{0,6},{2,0},{4,2},{6,4},{1,7},{3,1},{5,3},{7,5},{8,14},{10,8},{12,... | collective-permute-start | bytes 393224 | tf_op jit(solution)/shard_map/ppermute | solution.py:479
  102.0 5.6 %collective-permute-start.14 = (bf16[512,128]{1,0:T(8,128)(2,1)}, bf16[512,128]{1,0:T(8,128)(2,1)S(1)}, u32[]{:S(2)}, u32[]{:S(2)}) collective-permute-start(bf16[512,128]{1,0:T(8,128)(2,1)} %get-tuple-element.76), channel_id=1, source_target_pairs={{0,4},{2,6},{4,0},{6,2},{1,5},{3,7},{5,1},{7,3},{8,12},{10,14},{12... | collective-permute-start | bytes 393224 | tf_op jit(solution)/shard_map/ppermute | solution.py:479
  103.2 7.8 %collective-permute-start.13 = (bf16[512,128]{1,0:T(8,128)(2,1)}, bf16[512,128]{1,0:T(8,128)(2,1)S(1)}, u32[]{:S(2)}, u32[]{:S(2)}) collective-permute-start(bf16[512,128]{1,0:T(8,128)(2,1)} %get-tuple-element.76), channel_id=1, source_target_pairs={{0,2},{2,4},{4,6},{6,0},{1,3},{3,5},{5,7},{7,1},{8,10},{10,12},{12... | collective-permute-start | bytes 393224 | tf_op jit(solution)/shard_map/ppermute | solution.py:479
  110.9 55.4 %copy-start = (s32[64]{0:T(128)S(1)}, s32[64]{0:T(128)}, u32[]{:S(2)}) copy-start(s32[64]{0:T(128)} %get-tuple-element.55.refs_0_.slot_of) | copy-start | bytes 772
  112.7 33.8 %collective-permute-start.16 = (bf16[4,512,128]{2,1,0:T(8,128)(2,1)}, bf16[4,512,128]{2,1,0:T(8,128)(2,1)}, u32[]{:S(2)}, u32[]{:S(2)}) collective-permute-start(bf16[4,512,128]{2,1,0:T(8,128)(2,1)} %pad_maximum_fusion.own), channel_id=1, source_target_pairs={{0,1},{1,0},{2,3},{3,2},{4,5},{5,4},{6,7},{7,6},{8,9},{9,8},{10,11... | collective-permute-start | bytes 1572872 | tf_op jit(solution)/shard_map/ppermute | solution.py:515
  114.2 9.2 %collective-permute-start.26 = (bf16[256,128]{1,0:T(8,128)(2,1)S(1)}, bf16[256,128]{1,0:T(8,128)(2,1)S(1)}, u32[]{:S(2)}, u32[]{:S(2)}) collective-permute-start(bf16[256,128]{1,0:T(8,128)(2,1)S(1)} %get-tuple-element.86.refs_0_), channel_id=1, source_target_pairs={{0,56},{8,0},{16,8},{24,16},{32,24},{40,32},{48,40},{56,48},{1,57}... | collective-permute-start | bytes 196616 | tf_op jit(solution)/shard_map/ppermute | solution.py:482
  116.8 6.6 %collective-permute-start.25 = (bf16[256,128]{1,0:T(8,128)(2,1)S(1)}, bf16[256,128]{1,0:T(8,128)(2,1)S(1)}, u32[]{:S(2)}, u32[]{:S(2)}) collective-permute-start(bf16[256,128]{1,0:T(8,128)(2,1)S(1)} %get-tuple-element.86.refs_0_), channel_id=1, source_target_pairs={{0,48},{8,56},{16,0},{24,8},{32,16},{40,24},{48,32},{56,40},{1,49}... | collective-permute-start | bytes 196616 | tf_op jit(solution)/shard_map/ppermute | solution.py:482
  118.9 7.7 %collective-permute-start.24 = (bf16[256,128]{1,0:T(8,128)(2,1)S(1)}, bf16[256,128]{1,0:T(8,128)(2,1)S(1)}, u32[]{:S(2)}, u32[]{:S(2)}) collective-permute-start(bf16[256,128]{1,0:T(8,128)(2,1)S(1)} %get-tuple-element.86.refs_0_), channel_id=1, source_target_pairs={{0,40},{8,48},{16,56},{24,0},{32,8},{40,16},{48,24},{56,32},{1,41}... | collective-permute-start | bytes 196616 | tf_op jit(solution)/shard_map/ppermute | solution.py:482
  120.1 7.8 %collective-permute-start.23 = (bf16[256,128]{1,0:T(8,128)(2,1)S(1)}, bf16[256,128]{1,0:T(8,128)(2,1)S(1)}, u32[]{:S(2)}, u32[]{:S(2)}) collective-permute-start(bf16[256,128]{1,0:T(8,128)(2,1)S(1)} %get-tuple-element.86.refs_0_), channel_id=1, source_target_pairs={{0,32},{8,40},{16,48},{24,56},{32,0},{40,8},{48,16},{56,24},{1,33}... | collective-permute-start | bytes 196616 | tf_op jit(solution)/shard_map/ppermute | solution.py:482
  123.4 9.6 %collective-permute-start.22 = (bf16[256,128]{1,0:T(8,128)(2,1)S(1)}, bf16[256,128]{1,0:T(8,128)(2,1)S(1)}, u32[]{:S(2)}, u32[]{:S(2)}) collective-permute-start(bf16[256,128]{1,0:T(8,128)(2,1)S(1)} %get-tuple-element.86.refs_0_), channel_id=1, source_target_pairs={{0,24},{8,32},{16,40},{24,48},{32,56},{40,0},{48,8},{56,16},{1,25}... | collective-permute-start | bytes 196616 | tf_op jit(solution)/shard_map/ppermute | solution.py:482
  123.4 12.3 %collective-permute-start.21 = (bf16[256,128]{1,0:T(8,128)(2,1)S(1)}, bf16[256,128]{1,0:T(8,128)(2,1)S(1)}, u32[]{:S(2)}, u32[]{:S(2)}) collective-permute-start(bf16[256,128]{1,0:T(8,128)(2,1)S(1)} %get-tuple-element.86.refs_0_), channel_id=1, source_target_pairs={{0,16},{8,24},{16,32},{24,40},{32,48},{40,56},{48,0},{56,8},{1,17}... | collective-permute-start | bytes 196616 | tf_op jit(solution)/shard_map/ppermute | solution.py:482
  126.7 9.8 %collective-permute-start.20 = (bf16[256,128]{1,0:T(8,128)(2,1)S(1)}, bf16[256,128]{1,0:T(8,128)(2,1)S(1)}, u32[]{:S(2)}, u32[]{:S(2)}) collective-permute-start(bf16[256,128]{1,0:T(8,128)(2,1)S(1)} %get-tuple-element.86.refs_0_), channel_id=1, source_target_pairs={{0,8},{8,16},{16,24},{24,32},{32,40},{40,48},{48,56},{56,0},{1,9},... | collective-permute-start | bytes 196616 | tf_op jit(solution)/shard_map/ppermute | solution.py:482
  137.8 6.9 %collective-permute-start.27 = (bf16[1024,128]{1,0:T(8,128)(2,1)S(1)}, bf16[1024,128]{1,0:T(8,128)(2,1)S(1)}, u32[]{:S(2)}, u32[]{:S(2)}) collective-permute-start(bf16[1024,128]{1,0:T(8,128)(2,1)S(1)} %get-tuple-element.88), channel_id=1, source_target_pairs={{0,192},{64,0},{128,64},{192,128},{1,193},{65,1},{129,65},{193,129... | collective-permute-start | bytes 786440 | tf_op jit(solution)/shard_map/ppermute | solution.py:482
  139.8 14.2 %collective-permute-start.28 = (bf16[1024,128]{1,0:T(8,128)(2,1)S(1)}, bf16[1024,128]{1,0:T(8,128)(2,1)S(1)}, u32[]{:S(2)}, u32[]{:S(2)}) collective-permute-start(bf16[1024,128]{1,0:T(8,128)(2,1)S(1)} %get-tuple-element.89), channel_id=1, source_target_pairs={{0,128},{64,192},{128,0},{192,64},{1,129},{65,193},{129,1},{193,65... | collective-permute-start | bytes 786440 | tf_op jit(solution)/shard_map/ppermute | solution.py:482
  140.7 16.3 %collective-permute-start.29 = (bf16[1024,128]{1,0:T(8,128)(2,1)S(1)}, bf16[1024,128]{1,0:T(8,128)(2,1)S(1)}, u32[]{:S(2)}, u32[]{:S(2)}) collective-permute-start(bf16[1024,128]{1,0:T(8,128)(2,1)S(1)} %get-tuple-element.90), channel_id=1, source_target_pairs={{0,64},{64,128},{128,192},{192,0},{1,65},{65,129},{129,193},{193,1... | collective-permute-start | bytes 786440 | tf_op jit(solution)/shard_map/ppermute | solution.py:482
  142.0 15.0 %collective-permute-start.17 = (bf16[1024,128]{1,0:T(8,128)(2,1)S(1)}, bf16[1024,128]{1,0:T(8,128)(2,1)S(1)}, u32[]{:S(2)}, u32[]{:S(2)}) collective-permute-start(bf16[1024,128]{1,0:T(8,128)(2,1)S(1)} %get-tuple-element.83), channel_id=1, source_target_pairs={{0,192},{64,0},{128,64},{192,128},{1,193},{65,1},{129,65},{193,129... | collective-permute-start | bytes 786440 | tf_op jit(solution)/shard_map/ppermute | solution.py:482
  144.7 13.5 %collective-permute-start.18 = (bf16[1024,128]{1,0:T(8,128)(2,1)S(1)}, bf16[1024,128]{1,0:T(8,128)(2,1)S(1)}, u32[]{:S(2)}, u32[]{:S(2)}) collective-permute-start(bf16[1024,128]{1,0:T(8,128)(2,1)S(1)} %get-tuple-element.84), channel_id=1, source_target_pairs={{0,128},{64,192},{128,0},{192,64},{1,129},{65,193},{129,1},{193,65... | collective-permute-start | bytes 786440 | tf_op jit(solution)/shard_map/ppermute | solution.py:482
  146.5 19.9 %collective-permute-start.19 = (bf16[1024,128]{1,0:T(8,128)(2,1)S(1)}, bf16[1024,128]{1,0:T(8,128)(2,1)S(1)}, u32[]{:S(2)}, u32[]{:S(2)}) collective-permute-start(bf16[1024,128]{1,0:T(8,128)(2,1)S(1)} %get-tuple-element.85), channel_id=1, source_target_pairs={{0,64},{64,128},{128,192},{192,0},{1,65},{65,129},{129,193},{193,1... | collective-permute-start | bytes 786440 | tf_op jit(solution)/shard_map/ppermute | solution.py:482
  167.5 2.2 %collective-permute-start.34 = (bf16[4,32,16,128]{3,2,1,0:T(8,128)(2,1)S(1)}, bf16[4,32,16,128]{3,2,1,0:T(8,128)(2,1)S(1)}, u32[]{:S(2)}, u32[]{:S(2)}) collective-permute-start(bf16[4,32,16,128]{3,2,1,0:T(8,128)(2,1)S(1)} %get-tuple-element.99), channel_id=1, source_target_pairs={{0,1},{1,0},{2,3},{3,2},{4,5},{5,4},{6,7},{7,6},{8,9},{9,8},{10,11... | collective-permute-start | bytes 1572872 | tf_op jit(solution)/shard_map/ppermute | solution.py:521
  169.2 3.9 %collective-permute-start.30 = (bf16[4,32,16,128]{3,2,1,0:T(8,128)(2,1)S(1)}, bf16[4,32,16,128]{3,2,1,0:T(8,128)(2,1)S(1)}, u32[]{:S(2)}, u32[]{:S(2)}) collective-permute-start(bf16[4,32,16,128]{3,2,1,0:T(8,128)(2,1)S(1)} %get-tuple-element.93), channel_id=1, source_target_pairs={{0,1},{1,0},{2,3},{3,2},{4,5},{5,4},{6,7},{7,6},{8,9},{9,8},{10,11... | collective-permute-start | bytes 1572872 | tf_op jit(solution)/shard_map/ppermute | solution.py:521
  169.8 8.3 %collective-permute-start.35 = (bf16[32,16,128]{2,1,0:T(8,128)(2,1)S(1)}, bf16[32,16,128]{2,1,0:T(8,128)(2,1)S(1)}, u32[]{:S(2)}, u32[]{:S(2)}) collective-permute-start(bf16[32,16,128]{2,1,0:T(8,128)(2,1)S(1)} %get-tuple-element.101), channel_id=1, source_target_pairs={{0,2},{2,4},{4,6},{6,0},{1,3},{3,5},{5,7},{7,1},{8,10},{10,12},{12... | collective-permute-start | bytes 393224 | tf_op jit(solution)/shard_map/ppermute | solution.py:479
  169.9 8.3 %collective-permute-start.36 = (bf16[32,16,128]{2,1,0:T(8,128)(2,1)S(1)}, bf16[32,16,128]{2,1,0:T(8,128)(2,1)S(1)}, u32[]{:S(2)}, u32[]{:S(2)}) collective-permute-start(bf16[32,16,128]{2,1,0:T(8,128)(2,1)S(1)} %get-tuple-element.102), channel_id=1, source_target_pairs={{0,4},{2,6},{4,0},{6,2},{1,5},{3,7},{5,1},{7,3},{8,12},{10,14},{12... | collective-permute-start | bytes 393224 | tf_op jit(solution)/shard_map/ppermute | solution.py:479
  171.4 8.1 %collective-permute-start.37 = (bf16[32,16,128]{2,1,0:T(8,128)(2,1)S(1)}, bf16[32,16,128]{2,1,0:T(8,128)(2,1)S(1)}, u32[]{:S(2)}, u32[]{:S(2)}) collective-permute-start(bf16[32,16,128]{2,1,0:T(8,128)(2,1)S(1)} %get-tuple-element.103), channel_id=1, source_target_pairs={{0,6},{2,0},{4,2},{6,4},{1,7},{3,1},{5,3},{7,5},{8,14},{10,8},{12,... | collective-permute-start | bytes 393224 | tf_op jit(solution)/shard_map/ppermute | solution.py:479
  173.3 11.0 %collective-permute-start.31 = (bf16[32,16,128]{2,1,0:T(8,128)(2,1)S(1)}, bf16[32,16,128]{2,1,0:T(8,128)(2,1)S(1)}, u32[]{:S(2)}, u32[]{:S(2)}) collective-permute-start(bf16[32,16,128]{2,1,0:T(8,128)(2,1)S(1)} %get-tuple-element.95), channel_id=1, source_target_pairs={{0,2},{2,4},{4,6},{6,0},{1,3},{3,5},{5,7},{7,1},{8,10},{10,12},{12... | collective-permute-start | bytes 393224 | tf_op jit(solution)/shard_map/ppermute | solution.py:479
  173.4 10.9 %collective-permute-start.32 = (bf16[32,16,128]{2,1,0:T(8,128)(2,1)S(1)}, bf16[32,16,128]{2,1,0:T(8,128)(2,1)S(1)}, u32[]{:S(2)}, u32[]{:S(2)}) collective-permute-start(bf16[32,16,128]{2,1,0:T(8,128)(2,1)S(1)} %get-tuple-element.96), channel_id=1, source_target_pairs={{0,4},{2,6},{4,0},{6,2},{1,5},{3,7},{5,1},{7,3},{8,12},{10,14},{12... | collective-permute-start | bytes 393224 | tf_op jit(solution)/shard_map/ppermute | solution.py:479
  178.2 6.3 %collective-permute-start.33 = (bf16[32,16,128]{2,1,0:T(8,128)(2,1)S(1)}, bf16[32,16,128]{2,1,0:T(8,128)(2,1)S(1)}, u32[]{:S(2)}, u32[]{:S(2)}) collective-permute-start(bf16[32,16,128]{2,1,0:T(8,128)(2,1)S(1)} %get-tuple-element.97), channel_id=1, source_target_pairs={{0,6},{2,0},{4,2},{6,4},{1,7},{3,1},{5,3},{7,5},{8,14},{10,8},{12,... | collective-permute-start | bytes 393224 | tf_op jit(solution)/shard_map/ppermute | solution.py:479
